TPU v7x, 32 devices: a whole 2x2x4 slice. The times are simulated.
32 devices in a mesh: ctx: 16 (over z, y, x), head: 2 (over core).
Axes of the slice: x: 2, y: 2, z: 4, core: 2. Of those that a mesh axis runs over, the one named last changes fastest.
Arguments:
- queries: bfloat16 [512, 8192], P('ctx', 'head'), may hold values from -6 to 6
- cache_keys: bfloat16 [16384, 8, 128], P('ctx', 'head'), may hold values from -6 to 6
- cache_values: bfloat16 [16384, 8, 128], P('ctx', 'head'), may hold values from -6 to 6
- vertical_blocks: int32 [64, 8], P('head'), may hold values from 0 to 127, as said below
- slash_offsets: int32 [64, 48], P('head'), may hold values from 0 to 127, as said below
- out_weight: bfloat16 [8192, 8192], P('head', 'ctx'), may hold values from -0.0625 to 0.0625
Outputs:
- projected: bfloat16 [512, 8192], P('head', 'ctx')
Inputs may be any that keep to these rules, and one draw needn't show every extreme that they name: `vertical_blocks`: every head's list holds block 0; entries may repeat, and a block counts once however often it is named. `slash_offsets`: every head's list holds offset 0; entries may repeat, and a block counts once however often it is reached.
All inputs are finite; a program needn't handle non-finite values.
Results may differ from a plain program's by a relative error of at most 0.007.
Values may be sent and summed in bfloat16 or wider, within the bound.
No kernel may reach another device: no remote copies, remote signals or barrier semaphores. Data moves between devices by JAX's collectives and lax.ppermute only.
A program may use at most 128 MiB of HBM per device.

v0:
```python
from functools import partial
import math

import jax
import jax.numpy as jnp
from jax import lax
from jax.experimental import pallas as pl
from jax.experimental.pallas import tpu as pltpu
from jax.sharding import PartitionSpec as P


BLOCK = 128
NEG_FILL = -1e30
CHUNK = 8
STEP = 2
VMEM_LIMIT = 20 << 20


def attention_kernel(
    turn_ref, count_ref, diag_ref, klist_ref, slist_ref, table_ref, k_ref, v_ref, *refs, scale2, list_len, pieces,
):
    *q_refs, o_ref, q_ref, even_sc, odd_sc, diag_sc = refs
    width = k_ref.shape[1]
    heads = q_ref.shape[1] // width
    turn = turn_ref[0]
    piece_rows = BLOCK // pieces
    for i in range(pieces):
        place = table_ref[turn * pieces + i]
        for j, ref in enumerate(q_refs):

            @pl.when(place // pieces == j)
            def _(i=i, j=j, ref=ref, place=place):
                start = pl.multiple_of((place - j * pieces) * piece_rows, piece_rows)
                q_ref[i * piece_rows : (i + 1) * piece_rows, :] = ref[pl.ds(start, piece_rows), :]

    diag = diag_ref[turn]
    bufs = (even_sc, odd_sc)

    def block_of(ref, index):
        return ref[pl.ds(pl.multiple_of(index * BLOCK, BLOCK), BLOCK), :]

    def scores_of(keys, h):
        q = q_ref[:, h * width : (h + 1) * width]
        s = lax.dot_general(q, keys, (((1,), (1,)), ((), ())), preferred_element_type=jnp.float32)
        return s * scale2

    for buf in bufs:
        buf[list_len] = jnp.full((BLOCK, BLOCK), NEG_FILL, jnp.float32)

    @pl.when(diag >= 0)
    def _():
        keys = block_of(k_ref, diag)
        causal = lax.broadcasted_iota(jnp.int32, (BLOCK, BLOCK), 1) <= lax.broadcasted_iota(
            jnp.int32, (BLOCK, BLOCK), 0
        )
        for h in range(heads):
            diag_sc[h] = jnp.where(causal, scores_of(keys, h), NEG_FILL)

    @pl.when(diag < 0)
    def _():
        diag_sc[...] = jnp.full(diag_sc.shape, NEG_FILL, jnp.float32)

    diag_values = block_of(v_ref, jnp.maximum(diag, 0))
    counts = [count_ref[turn * heads + h] for h in range(heads)]
    chunks = [(c + CHUNK - 1) // CHUNK for c in counts]

    def score_part(h, t, u, top):
        base = (turn * heads + h) * list_len + t * CHUNK + u
        keys = jnp.concatenate([block_of(k_ref, klist_ref[base + i]) for i in range(STEP)], axis=0)
        s = scores_of(keys, h)
        for i in range(STEP):
            part = s[:, i * BLOCK : (i + 1) * BLOCK]
            bufs[h % 2][t * CHUNK + u + i] = part
            top = jnp.maximum(top, part)
        return top

    def value_part(h, t, u, m, total, acc):
        base = (turn * heads + h) * list_len + t * CHUNK + u
        values = jnp.concatenate([block_of(v_ref, klist_ref[base + i]) for i in range(STEP)], axis=0)
        parts = [jnp.exp2(bufs[h % 2][slist_ref[base + i]] - m) for i in range(STEP)]
        for p in parts:
            total = total + p
        p = jnp.concatenate([p.astype(jnp.bfloat16) for p in parts], axis=1)
        return total, acc + jnp.dot(p, values, preferred_element_type=jnp.float32)

    top_start = jnp.full((BLOCK, BLOCK), NEG_FILL, jnp.float32)

    def first(t, top):
        for u in range(0, CHUNK, STEP):
            top = score_part(0, t, u, top)
        return top

    top = lax.fori_loop(0, chunks[0], first, top_start)
    lane = lax.broadcasted_iota(jnp.int32, (BLOCK, BLOCK), 1)
    lse = jnp.full((BLOCK, BLOCK), NEG_FILL, jnp.float32)
    for h in range(heads):
        top = jnp.maximum(jnp.where(counts[h] > 0, top, NEG_FILL), diag_sc[h])
        m = jnp.max(top, axis=1, keepdims=True)
        total = jnp.exp2(diag_sc[h] - m)
        total = jnp.where(diag >= 0, total, 0.0)
        acc = jnp.dot(total.astype(jnp.bfloat16), diag_values, preferred_element_type=jnp.float32)
        if h + 1 < heads:

            def both(t, carry, h=h, m=m):
                top, total, acc = carry
                for u in range(0, CHUNK, STEP):
                    top = score_part(h + 1, t, u, top)
                    total, acc = value_part(h, t, u, m, total, acc)
                return top, total, acc

            top, total, acc = lax.fori_loop(
                0, jnp.maximum(chunks[h], chunks[h + 1]), both, (top_start, total, acc)
            )
        else:

            def last(t, carry, h=h, m=m):
                for u in range(0, CHUNK, STEP):
                    carry = value_part(h, t, u, m, *carry)
                return carry

            total, acc = lax.fori_loop(0, chunks[h], last, (total, acc))
        total = jnp.sum(total, axis=1, keepdims=True)
        seen = total > 0.0
        safe = jnp.where(seen, total, 1.0)
        o_ref[:, h * width : (h + 1) * width] = (acc / safe).astype(o_ref.dtype)
        mine = (lane == h) | (lane == heads + h) | (lane == 2 * heads + h)
        lse = jnp.where(mine & seen, m + jnp.log2(safe), lse)
    high = lse.astype(jnp.bfloat16)
    rest = lse - high.astype(jnp.float32)
    middle = rest.astype(jnp.bfloat16)
    low = rest - middle.astype(jnp.float32)
    packed = jnp.where(lane < heads, high.astype(jnp.float32), jnp.where(lane < 2 * heads, middle.astype(jnp.float32), low))
    o_ref[:, heads * width :] = packed.astype(o_ref.dtype)


def block_attention(turn, meta, table, q_parts, keys, values):
    count, diag, klist, slist = meta
    turns = diag.shape[0]
    heads = count.shape[0] // turns
    width = keys.shape[1]
    list_len = klist.shape[0] // count.shape[0]
    smem = pl.BlockSpec(memory_space=pltpu.SMEM)
    vmem = pl.BlockSpec(memory_space=pltpu.VMEM)
    return pl.pallas_call(
        partial(
            attention_kernel,
            scale2=float(width) ** -0.5 * math.log2(math.e),
            list_len=list_len,
            pieces=table.shape[0] // turns,
        ),
        out_shape=jax.ShapeDtypeStruct((BLOCK, heads * width + BLOCK), jnp.bfloat16),
        in_specs=[smem] * 6 + [vmem] * (2 + len(q_parts)),
        out_specs=vmem,
        scratch_shapes=[
            pltpu.VMEM((BLOCK, heads * width), jnp.bfloat16),
            pltpu.VMEM((list_len + 1, BLOCK, BLOCK), jnp.float32),
            pltpu.VMEM((list_len + 1, BLOCK, BLOCK), jnp.float32),
            pltpu.VMEM((heads, BLOCK, BLOCK), jnp.float32),
        ],
        compiler_params=pltpu.CompilerParams(vmem_limit_bytes=VMEM_LIMIT),
        name="block_attention",
    )(jnp.full((1,), turn, jnp.int32), count, diag, klist, slist, table, keys, values, *q_parts)


def combine_kernel(*refs):
    outs, att_ref = refs[:-1], refs[-1]
    feats = att_ref.shape[1]
    width = outs[0].shape[1] - feats
    heads = feats // width
    lse = []
    for ref in outs:
        x = ref[:, feats:].astype(jnp.float32)
        lse.append(x + pltpu.roll(x, width - heads, 1) + pltpu.roll(x, width - 2 * heads, 1))
    top = lse[0]
    for x in lse[1:]:
        top = jnp.maximum(top, x)
    weight = [jnp.exp2(x - top) for x in lse]
    total = weight[0]
    for x in weight[1:]:
        total = total + x
    inverse = 1.0 / total
    weight = [x * inverse for x in weight]
    for h in range(heads):
        cols = slice(h * width, (h + 1) * width)
        mixed = outs[0][:, cols].astype(jnp.float32) * weight[0][:, h : h + 1]
        for ref, x in zip(outs[1:], weight[1:]):
            mixed = mixed + ref[:, cols].astype(jnp.float32) * x[:, h : h + 1]
        att_ref[:, cols] = mixed.astype(att_ref.dtype)


def combine(outs, feats):
    return pl.pallas_call(
        combine_kernel,
        out_shape=jax.ShapeDtypeStruct((outs[0].shape[0], feats), jnp.bfloat16),
        compiler_params=pltpu.CompilerParams(vmem_limit_bytes=VMEM_LIMIT),
        name="combine",
    )(*outs)


def project_kernel(order_ref, *refs, blocks, parts):
    *refs, away_ref, own_ref, rows_sc = refs
    att_refs, weight_refs = refs[:parts], refs[parts:]
    rows = blocks * BLOCK
    for i in range(parts):
        for k, ref in enumerate(att_refs):

            @pl.when(order_ref[i] == k)
            def _(i=i, ref=ref):
                rows_sc[i * BLOCK : (i + 1) * BLOCK, :] = ref[...]

    for m, ref in enumerate(weight_refs):
        out = jnp.dot(rows_sc[rows:, :], ref[...], preferred_element_type=jnp.float32)
        away_ref[m] = out.reshape(-1, rows, out.shape[1]).astype(away_ref.dtype)
        own_ref[m] = jnp.dot(rows_sc[:rows, :], ref[...], preferred_element_type=jnp.float32)


def project(order, blocks, atts, weights):
    rows, parts, plane = blocks * BLOCK, len(atts), len(weights)
    columns = weights[0].shape[1]
    vmem = pl.BlockSpec(memory_space=pltpu.VMEM)
    return pl.pallas_call(
        partial(project_kernel, blocks=blocks, parts=parts),
        out_shape=(
            jax.ShapeDtypeStruct((plane, parts // blocks - 1, rows, columns), jnp.bfloat16),
            jax.ShapeDtypeStruct((plane, rows, columns), jnp.float32),
        ),
        in_specs=[pl.BlockSpec(memory_space=pltpu.SMEM)] + [vmem] * (parts + plane),
        out_specs=(vmem, vmem),
        scratch_shapes=[pltpu.VMEM((parts * BLOCK, atts[0].shape[1]), jnp.bfloat16)],
        compiler_params=pltpu.CompilerParams(vmem_limit_bytes=VMEM_LIMIT),
        name="project",
    )(order, *atts, *weights)


def block_lists(vertical, slash, query_blocks, ids):
    local_blocks = ids.shape[0]
    offsets = query_blocks[:, None] - ids[None, :]
    vertical_hit = jnp.any(vertical[:, :, None] == ids[None, None, :], axis=1)
    slash_hit = jnp.any(slash[None, :, :, None] == offsets[:, None, None, :], axis=2)
    picked = (vertical_hit[None] | slash_hit) & (offsets > 0)[:, None, :]
    picked = picked.astype(jnp.int32)
    order = jnp.arange(local_blocks, dtype=jnp.int32)
    rank = jnp.sum(picked[:, :, None, :] * (order[None, :] < order[:, None]), axis=3)
    count = jnp.sum(picked, axis=2)
    list_len = -(-local_blocks // CHUNK) * CHUNK
    slot = jnp.arange(list_len, dtype=jnp.int32)
    wanted = jnp.where(slot[None, None, :] < count[:, :, None], slot[None, None, :], 0)
    match = picked[:, :, None, :] * (rank[:, :, None, :] == wanted[:, :, :, None])
    klist = jnp.sum(match * order, axis=3)
    slist = jnp.where(slot[None, None, :] < count[:, :, None], slot[None, None, :], list_len)
    own = query_blocks[:, None] == ids[None, :]
    diag = jnp.where(jnp.any(own, axis=1), jnp.sum(own * order, axis=1), -1).astype(jnp.int32)
    return count.reshape(-1), diag, klist.reshape(-1), slist.reshape(-1)


def plane_body(queries, cache_keys, cache_values, vertical_blocks, slash_offsets, out_weight):
    ctx_count = lax.axis_size("ctx")
    core_count = lax.axis_size("head")
    place = lax.axis_index("ctx")
    core = lax.axis_index("head")
    local_len, plane, width = cache_keys.shape
    lines = ctx_count // plane
    bits = plane.bit_length() - 1
    heads = vertical_blocks.shape[0] // plane
    feats = heads * width
    all_blocks = local_len // BLOCK * ctx_count

    def line_mask(k):
        return k << bits

    def plane_of(x):
        return x & (plane - 1)

    def line_of(x):
        return x >> bits

    mine, line = plane_of(place), line_of(place)

    def swap(x, mask):
        return lax.ppermute(x, "ctx", [(i, i ^ mask) for i in range(ctx_count)]) if mask else x

    q_own = jnp.concatenate(
        [
            swap(lax.dynamic_slice_in_dim(queries, (mine ^ m) * feats, feats, 1), m)
            for m in range(plane)
        ],
        axis=0,
    )

    def by_head(cache):
        heads_first = lax.optimization_barrier(jnp.transpose(cache, (1, 0, 2)))
        moved = [
            swap(lax.dynamic_index_in_dim(heads_first, mine ^ m, 0, keepdims=False), m)
            for m in range(plane)
        ]
        return jnp.concatenate(moved, axis=0)

    q_parts = []
    for k in range(lines):
        q_parts.append(swap(q_own, line_mask(k)))
    keys = by_head(cache_keys)
    values = by_head(cache_values)

    turns = line ^ jnp.arange(lines, dtype=jnp.int32)
    meta = block_lists(
        lax.dynamic_slice_in_dim(vertical_blocks, mine * heads, heads, 0),
        lax.dynamic_slice_in_dim(slash_offsets, mine * heads, heads, 0),
        all_blocks - lines + turns,
        jnp.concatenate(
            [
                (place ^ m) * (local_len // BLOCK)
                + jnp.arange(local_len // BLOCK, dtype=jnp.int32)
                for m in range(plane)
            ]
        ),
    )
    source = (turns[:, None] * plane + jnp.arange(plane, dtype=jnp.int32)[None, :]) ^ place
    table = (line_of(source) * plane + plane_of(source)).reshape(-1)
    share = lines // core_count
    steps = jnp.arange(core_count, dtype=jnp.int32)
    half = jnp.where(core + steps >= core_count, core + steps - core_count, core + steps)
    order = (half[:, None] * share + jnp.arange(share, dtype=jnp.int32)[None, :]).reshape(-1) ^ line

    keys, values, weight, table, order, meta, q_parts = lax.optimization_barrier(
        (keys, values, out_weight, table, order, meta, q_parts)
    )
    slabs = [lax.dynamic_slice_in_dim(weight, (mine ^ m) * feats, feats, 0) for m in range(plane)]
    weights = []
    for m in range(plane):
        weights.append(swap(slabs[m], m))

    outs = [None] * lines
    for k in reversed(range(lines)):
        o = block_attention(k, meta, table, q_parts, keys, values)
        if k:
            keys, o = lax.optimization_barrier((keys, o))
        outs[k] = swap(o, line_mask(k))
    att = combine(outs, feats)
    atts = [swap(att, line_mask(k)) for k in range(lines)]

    away, sums = project(order, share, atts, weights)
    for step in range(1, core_count):
        got = lax.ppermute(away[:, step - 1], "head", [(a, (a + step) % core_count) for a in range(core_count)])
        sums = sums + got.astype(jnp.float32)
    result = sums[0]
    for m in range(1, plane):
        result = result + swap(sums[m].astype(jnp.bfloat16), m).astype(jnp.float32)
    return result.astype(jnp.bfloat16)


def general_body(queries, cache_keys, cache_values, vertical_blocks, slash_offsets, out_weight):
    ctx_count = lax.axis_size("ctx")
    place = lax.axis_index("ctx")
    local_len, kv_local, width = cache_keys.shape
    heads = vertical_blocks.shape[0] // kv_local
    feats = heads * width
    q_whole = lax.all_gather(queries, "ctx", axis=0, tiled=True)
    q_blocks = q_whole.shape[0] // BLOCK
    local_blocks = local_len // BLOCK
    query_blocks = local_blocks * ctx_count - q_blocks + jnp.arange(q_blocks, dtype=jnp.int32)
    attention = []
    for g in range(kv_local):
        meta = block_lists(
            vertical_blocks[g * heads : (g + 1) * heads],
            slash_offsets[g * heads : (g + 1) * heads],
            query_blocks,
            place * local_blocks + jnp.arange(local_blocks, dtype=jnp.int32),
        )
        table = jnp.zeros((q_blocks,), jnp.int32)
        outs = []
        for b in range(q_blocks):
            q = q_whole[b * BLOCK : (b + 1) * BLOCK, g * feats : (g + 1) * feats]
            outs.append(block_attention(b, meta, table, [q], cache_keys[:, g, :], cache_values[:, g, :]))
        out = jnp.concatenate(outs, axis=0)
        lse = jnp.sum(out[:, feats : feats + 3 * heads].astype(jnp.float32).reshape(-1, 3, heads), axis=1)
        out = out[:, :feats].reshape(-1, heads, width)
        factor = jnp.exp2(lse - lax.pmax(lse, "ctx"))
        out, total = lax.psum((out.astype(jnp.float32) * factor[:, :, None], factor), "ctx")
        attention.append((out / total[:, :, None]).astype(jnp.bfloat16).reshape(-1, feats))
    return lax.psum_scatter(
        jnp.dot(jnp.concatenate(attention, axis=1), out_weight, preferred_element_type=jnp.float32),
        "head",
        scatter_dimension=0,
        tiled=True,
    ).astype(jnp.bfloat16)


def body(queries, cache_keys, cache_values, vertical_blocks, slash_offsets, out_weight):
    ctx_count = lax.axis_size("ctx")
    lines = queries.shape[0] * ctx_count // BLOCK
    plane, cores = cache_keys.shape[1], lax.axis_size("head")
    powers = all(n & (n - 1) == 0 for n in (plane, lines, cores))
    fits = powers and plane * lines == ctx_count and lines % cores == 0 and lines > 1
    chosen = plane_body if fits else general_body
    return chosen(queries, cache_keys, cache_values, vertical_blocks, slash_offsets, out_weight)


def solution(mesh):
    return jax.shard_map(
        body,
        mesh=mesh,
        in_specs=(
            P("ctx", "head"),
            P("ctx", "head", None),
            P("ctx", "head", None),
            P("head", None),
            P("head", None),
            P("head", "ctx"),
        ),
        out_specs=P("head", "ctx"),
        check_vma=False,
    )
```

profile of v0, /device:TPU:0, one launch (start us, length us, event | category | flops | bytes accessed | tf_op | source)
XLA Modules:
  0.0 169.9 jit_solution(10223518808408180919)
XLA Ops:
  0.0 1.6 constant_dynamic-slice_fusion.7
  1.6 3.0 %collective-permute-start.6 = (bf16[32,1024]{1,0:T(8,128)(2,1)}, bf16[32,1024]{1,0:T(8,128)(2,1)}, u32[]{:S(2)}, u32[]{:S(2)}) collective-permute-start(bf16[32,1024]{1,0:T(8,128)(2,1)} %get-tuple-element.65), channel_id=1, source_target_pairs={{0,2},{2,0},{4,6},{6,4},{8,10},{10,8},{12,14},{14,12},{16,18},{18,... | collective-permute-start | bytes 196616 | tf_op jit(solution)/shard_map/ppermute | solution.py:280
  17.0 2.9 %collective-permute-start.5 = (bf16[1024,128]{1,0:T(8,128)(2,1)S(1)}, bf16[1024,128]{1,0:T(8,128)(2,1)S(1)}, u32[]{:S(2)}, u32[]{:S(2)}) collective-permute-start(bf16[1024,128]{1,0:T(8,128)(2,1)S(1)} %get-tuple-element.57), channel_id=1, source_target_pairs={{0,6},{2,4},{4,2},{6,0},{8,14},{10,12},{12,10},{14,8},{16,22},{18,... | collective-permute-start | bytes 786440 | tf_op jit(solution)/shard_map/ppermute | solution.py:280
  19.9 8.9 %collective-permute-done.7 = bf16[32,1024]{1,0:T(8,128)(2,1)S(1)} collective-permute-done((bf16[32,1024]{1,0:T(8,128)(2,1)}, bf16[32,1024]{1,0:T(8,128)(2,1)S(1)}, u32[]{:S(2)}, u32[]{:S(2)}) %collective-permute-start.7) | collective-permute-done | bytes 65568 | tf_op jit(solution)/shard_map/ppermute | solution.py:280
  31.7 3.6 %collective-permute-start.11 = (bf16[128,1024]{1,0:T(8,128)(2,1)S(1)}, bf16[128,1024]{1,0:T(8,128)(2,1)S(1)}, u32[]{:S(2)}, u32[]{:S(2)}) collective-permute-start(bf16[128,1024]{1,0:T(8,128)(2,1)S(1)} %pad_maximum_fusion.2.refs_0_), channel_id=1, source_target_pairs={{0,24},{2,26},{4,28},{6,30},{8,16},{10,18},{12,20},{14,22},{16,8},... | collective-permute-start | bytes 786440 | tf_op jit(solution)/shard_map/ppermute | solution.py:280
  38.7 4.0 %collective-permute-done.11.refs_3_ = bf16[128,1024]{1,0:T(8,128)(2,1)S(1)} collective-permute-done((bf16[128,1024]{1,0:T(8,128)(2,1)S(1)}, bf16[128,1024]{1,0:T(8,128)(2,1)S(1)}, u32[]{:S(2)}, u32[]{:S(2)}) %collective-permute-start.11) | collective-permute-done | bytes 262176 | tf_op jit(solution)/shard_map/ppermute | solution.py:280
  42.8 14.5 %collective-permute-done.10.refs_2_ = bf16[128,1024]{1,0:T(8,128)(2,1)S(1)} collective-permute-done((bf16[128,1024]{1,0:T(8,128)(2,1)S(1)}, bf16[128,1024]{1,0:T(8,128)(2,1)S(1)}, u32[]{:S(2)}, u32[]{:S(2)}) %collective-permute-start.10) | collective-permute-done | bytes 262176 | tf_op jit(solution)/shard_map/ppermute | solution.py:280
  57.3 6.0 %block_attention.4 = bf16[128,1152]{1,0:T(8,128)(2,1)S(1)} custom-call(s32[1]{0:T(128)} %constant.65.clone.1.turn_ref, s32[32]{0:T(128)S(1)} %reshape.124.count_ref, s32[4]{0:T(128)S(1)} %broadcast_select_fusion.diag_ref, s32[1024]{0:T(1024)S(1)} %reshape.125.klist_ref, s32[1024]{0:T(1024)S(1)} %compare_select_fusion.slist_ref, s32[16]{0:T(128)S(1)} %reshape.126.table_ref, ...), custom_call_target="tpu_custom_call" | custom-call | tf_op jit(solution)/shard_map/block_attention/pallas_call | solution.py:144
  63.2 6.0 %block_attention.5 = bf16[128,1152]{1,0:T(8,128)(2,1)S(1)} custom-call(s32[1]{0:T(128)} %constant.66.clone.1.turn_ref, s32[32]{0:T(128)S(1)} %reshape.124.count_ref, s32[4]{0:T(128)S(1)} %broadcast_select_fusion.diag_ref, s32[1024]{0:T(1024)S(1)} %reshape.125.klist_ref, s32[1024]{0:T(1024)S(1)} %compare_select_fusion.slist_ref, s32[16]{0:T(128)S(1)} %reshape.126.table_ref, ...), custom_call_target="tpu_custom_call" | custom-call | tf_op jit(solution)/shard_map/block_attention/pallas_call | solution.py:144
  69.2 6.1 %block_attention.6 = bf16[128,1152]{1,0:T(8,128)(2,1)S(1)} custom-call(s32[1]{0:T(128)} %constant.67.clone.1.turn_ref, s32[32]{0:T(128)S(1)} %reshape.124.count_ref, s32[4]{0:T(128)S(1)} %broadcast_select_fusion.diag_ref, s32[1024]{0:T(1024)S(1)} %reshape.125.klist_ref, s32[1024]{0:T(1024)S(1)} %compare_select_fusion.slist_ref, s32[16]{0:T(128)S(1)} %reshape.126.table_ref, ...), custom_call_target="tpu_custom_call" | custom-call | tf_op jit(solution)/shard_map/block_attention/pallas_call | solution.py:144
  75.7 3.3 %collective-permute-start.20 = (bf16[1024,512]{1,0:T(8,128)(2,1)S(1)}, bf16[1024,512]{1,0:T(8,128)(2,1)S(1)}, u32[]{:S(2)}, u32[]{:S(2)}) collective-permute-start(bf16[1024,512]{1,0:T(8,128)(2,1)S(1)} %get-tuple-element.49), channel_id=1, source_target_pairs={{0,6},{2,4},{4,2},{6,0},{8,14},{10,12},{12,10},{14,8},{16,22},{18,... | collective-permute-start | bytes 3145736 | tf_op jit(solution)/shard_map/ppermute | solution.py:280
  79.7 13.8 %collective-permute-start.13 = (bf16[128,1152]{1,0:T(8,128)(2,1)S(1)}, bf16[128,1152]{1,0:T(8,128)(2,1)S(1)}, u32[]{:S(2)}, u32[]{:S(2)}) collective-permute-start(bf16[128,1152]{1,0:T(8,128)(2,1)S(1)} %block_attention.5), channel_id=1, source_target_pairs={{0,16},{2,18},{4,20},{6,22},{8,24},{10,26},{12,28},{14,30},{16,0},... | collective-permute-start | bytes 884744 | tf_op jit(solution)/shard_map/ppermute | solution.py:280
  93.5 2.6 %collective-permute-start.14 = (bf16[128,1152]{1,0:T(8,128)(2,1)S(1)}, bf16[128,1152]{1,0:T(8,128)(2,1)S(1)}, u32[]{:S(2)}, u32[]{:S(2)}) collective-permute-start(bf16[128,1152]{1,0:T(8,128)(2,1)S(1)} %block_attention.4), channel_id=1, source_target_pairs={{0,24},{2,26},{4,28},{6,30},{8,16},{10,18},{12,20},{14,22},{16,8},... | collective-permute-start | bytes 884744 | tf_op jit(solution)/shard_map/ppermute | solution.py:280
  96.1 6.0 %block_attention.7.refs_0_ = bf16[128,1152]{1,0:T(8,128)(2,1)S(1)} custom-call(s32[1]{0:T(128)} %constant.64.clone.1.turn_ref, s32[32]{0:T(128)S(1)} %reshape.124.count_ref, s32[4]{0:T(128)S(1)} %broadcast_select_fusion.diag_ref, s32[1024]{0:T(1024)S(1)} %reshape.125.klist_ref, s32[1024]{0:T(1024)S(1)} %compare_select_fusion.slist_ref, ...), custom_call_target="tpu_custom_call" | custom-call | tf_op jit(solution)/shard_map/block_attention/pallas_call | solution.py:144
  102.1 10.1 %collective-permute-done.13.refs_2_ = bf16[128,1152]{1,0:T(8,128)(2,1)S(1)} collective-permute-done((bf16[128,1152]{1,0:T(8,128)(2,1)S(1)}, bf16[128,1152]{1,0:T(8,128)(2,1)S(1)}, u32[]{:S(2)}, u32[]{:S(2)}) %collective-permute-start.13) | collective-permute-done | bytes 294944 | tf_op jit(solution)/shard_map/ppermute | solution.py:280
  113.0 2.4 %collective-permute-start.17 = (bf16[128,1024]{1,0:T(8,128)(2,1)S(1)}, bf16[128,1024]{1,0:T(8,128)(2,1)S(1)}, u32[]{:S(2)}, u32[]{:S(2)}) collective-permute-start(bf16[128,1024]{1,0:T(8,128)(2,1)S(1)} %combine.1.refs_0_), channel_id=1, source_target_pairs={{0,24},{2,26},{4,28},{6,30},{8,16},{10,18},{12,20},{14,22},{16,8},... | collective-permute-start | bytes 786440 | tf_op jit(solution)/shard_map/ppermute | solution.py:280
  115.4 10.3 %collective-permute-start.16 = (bf16[128,1024]{1,0:T(8,128)(2,1)S(1)}, bf16[128,1024]{1,0:T(8,128)(2,1)S(1)}, u32[]{:S(2)}, u32[]{:S(2)}) collective-permute-start(bf16[128,1024]{1,0:T(8,128)(2,1)S(1)} %combine.1.refs_0_), channel_id=1, source_target_pairs={{0,16},{2,18},{4,20},{6,22},{8,24},{10,26},{12,28},{14,30},{16,0},... | collective-permute-start | bytes 786440 | tf_op jit(solution)/shard_map/ppermute | solution.py:280
  125.8 13.3 %collective-permute-start.15 = (bf16[128,1024]{1,0:T(8,128)(2,1)S(1)}, bf16[128,1024]{1,0:T(8,128)(2,1)S(1)}, u32[]{:S(2)}, u32[]{:S(2)}) collective-permute-start(bf16[128,1024]{1,0:T(8,128)(2,1)S(1)} %combine.1.refs_0_), channel_id=1, source_target_pairs={{0,8},{2,10},{4,12},{6,14},{8,0},{10,2},{12,4},{14,6},{16,24},{18,... | collective-permute-start | bytes 786440 | tf_op jit(solution)/shard_map/ppermute | solution.py:280
  139.1 3.0 %collective-permute-done.16.refs_2_ = bf16[128,1024]{1,0:T(8,128)(2,1)S(1)} collective-permute-done((bf16[128,1024]{1,0:T(8,128)(2,1)S(1)}, bf16[128,1024]{1,0:T(8,128)(2,1)S(1)}, u32[]{:S(2)}, u32[]{:S(2)}) %collective-permute-start.16) | collective-permute-done | bytes 262176 | tf_op jit(solution)/shard_map/ppermute | solution.py:280
  142.1 4.2 %collective-permute-done.15.refs_1_ = bf16[128,1024]{1,0:T(8,128)(2,1)S(1)} collective-permute-done((bf16[128,1024]{1,0:T(8,128)(2,1)S(1)}, bf16[128,1024]{1,0:T(8,128)(2,1)S(1)}, u32[]{:S(2)}, u32[]{:S(2)}) %collective-permute-start.15) | collective-permute-done | bytes 262176 | tf_op jit(solution)/shard_map/ppermute | solution.py:280
  146.4 3.1 %project.1 = (bf16[4,1,256,512]{3,2,1,0:T(8,128)(2,1)S(1)}, f32[4,256,512]{2,1,0:T(8,128)S(1)}) custom-call(s32[4]{0:T(128)S(1)} %xor.66.order_ref, bf16[128,1024]{1,0:T(8,128)(2,1)S(1)} %combine.1.refs_0_, bf16[128,1024]{1,0:T(8,128)(2,1)S(1)} %collective-permute-done.15.refs_1_, bf16[128,1024]{1,0:T(8,128)(2,1)S(1)} %collective-permute-done.16.refs_2_, ...), custom_call_target="tpu_custom_call" | custom-call | tf_op jit(solution)/shard_map/project/pallas_call | solution.py:221
  149.5 2.6 %collective-permute-done.21 = bf16[4,256,512]{2,1,0:T(8,128)(2,1)S(1)} collective-permute-done((bf16[4,256,512]{2,1,0:T(8,128)(2,1)S(1)}, bf16[4,256,512]{2,1,0:T(8,128)(2,1)S(1)}, u32[]{:S(2)}, u32[]{:S(2)}) %collective-permute-start.21) | collective-permute-done | bytes 1048608 | tf_op jit(solution)/shard_map/ppermute | solution.py:343
  156.3 5.7 %collective-permute-done.22 = bf16[256,512]{1,0:T(8,128)(2,1)S(1)} collective-permute-done((bf16[256,512]{1,0:T(8,128)(2,1)S(1)}, bf16[256,512]{1,0:T(8,128)(2,1)S(1)}, u32[]{:S(2)}, u32[]{:S(2)}) %collective-permute-start.22) | collective-permute-done | bytes 262176 | tf_op jit(solution)/shard_map/ppermute | solution.py:280
  162.0 5.6 %collective-permute-done.24 = bf16[256,512]{1,0:T(8,128)(2,1)S(1)} collective-permute-done((bf16[256,512]{1,0:T(8,128)(2,1)S(1)}, bf16[256,512]{1,0:T(8,128)(2,1)S(1)}, u32[]{:S(2)}, u32[]{:S(2)}) %collective-permute-start.24) | collective-permute-done | bytes 262176 | tf_op jit(solution)/shard_map/ppermute | solution.py:280
  (86 shorter events, 26.9 us)
Async XLA Ops:
  1.6 14.1 %collective-permute-start.6 = (bf16[32,1024]{1,0:T(8,128)(2,1)}, bf16[32,1024]{1,0:T(8,128)(2,1)}, u32[]{:S(2)}, u32[]{:S(2)}) collective-permute-start(bf16[32,1024]{1,0:T(8,128)(2,1)} %get-tuple-element.65), channel_id=1, source_target_pairs={{0,2},{2,0},{4,6},{6,4},{8,10},{10,8},{12,14},{14,12},{16,18},{18,... | collective-permute-start | bytes 196616 | tf_op jit(solution)/shard_map/ppermute | solution.py:280
  4.6 12.4 %collective-permute-start.8 = (bf16[32,1024]{1,0:T(8,128)(2,1)}, bf16[32,1024]{1,0:T(8,128)(2,1)}, u32[]{:S(2)}, u32[]{:S(2)}) collective-permute-start(bf16[32,1024]{1,0:T(8,128)(2,1)} %get-tuple-element.66), channel_id=1, source_target_pairs={{0,6},{2,4},{4,2},{6,0},{8,14},{10,12},{12,10},{14,8},{16,22},{18,... | collective-permute-start | bytes 196616 | tf_op jit(solution)/shard_map/ppermute | solution.py:280
  7.7 23.0 %collective-permute-start.2 = (bf16[1024,128]{1,0:T(8,128)(2,1)S(1)}, bf16[1024,128]{1,0:T(8,128)(2,1)S(1)}, u32[]{:S(2)}, u32[]{:S(2)}) collective-permute-start(bf16[1024,128]{1,0:T(8,128)(2,1)S(1)} %get-tuple-element.61), channel_id=1, source_target_pairs={{0,6},{2,4},{4,2},{6,0},{8,14},{10,12},{12,10},{14,8},{16,22},{18,... | collective-permute-start | bytes 786440 | tf_op jit(solution)/shard_map/ppermute | solution.py:280
  9.2 22.6 %collective-permute-start.1 = (bf16[1024,128]{1,0:T(8,128)(2,1)S(1)}, bf16[1024,128]{1,0:T(8,128)(2,1)}, u32[]{:S(2)}, u32[]{:S(2)}) collective-permute-start(bf16[1024,128]{1,0:T(8,128)(2,1)S(1)} %get-tuple-element.62), channel_id=1, source_target_pairs={{0,4},{2,6},{4,0},{6,2},{8,12},{10,14},{12,8},{14,10},{16,20},{18,... | collective-permute-start | bytes 786440 | tf_op jit(solution)/shard_map/ppermute | solution.py:280
  10.7 24.6 %collective-permute-start = (bf16[1024,128]{1,0:T(8,128)(2,1)S(1)}, bf16[1024,128]{1,0:T(8,128)(2,1)}, u32[]{:S(2)}, u32[]{:S(2)}) collective-permute-start(bf16[1024,128]{1,0:T(8,128)(2,1)S(1)} %get-tuple-element.63), channel_id=1, source_target_pairs={{0,2},{2,0},{4,6},{6,4},{8,10},{10,8},{12,14},{14,12},{16,18},{18,... | collective-permute-start | bytes 786440 | tf_op jit(solution)/shard_map/ppermute | solution.py:280
  15.7 13.0 %collective-permute-start.7 = (bf16[32,1024]{1,0:T(8,128)(2,1)}, bf16[32,1024]{1,0:T(8,128)(2,1)S(1)}, u32[]{:S(2)}, u32[]{:S(2)}) collective-permute-start(bf16[32,1024]{1,0:T(8,128)(2,1)} %get-tuple-element.67), channel_id=1, source_target_pairs={{0,4},{2,6},{4,0},{6,2},{8,12},{10,14},{12,8},{14,10},{16,20},{18,... | collective-permute-start | bytes 196616 | tf_op jit(solution)/shard_map/ppermute | solution.py:280
  17.0 19.4 %collective-permute-start.5 = (bf16[1024,128]{1,0:T(8,128)(2,1)S(1)}, bf16[1024,128]{1,0:T(8,128)(2,1)S(1)}, u32[]{:S(2)}, u32[]{:S(2)}) collective-permute-start(bf16[1024,128]{1,0:T(8,128)(2,1)S(1)} %get-tuple-element.57), channel_id=1, source_target_pairs={{0,6},{2,4},{4,2},{6,0},{8,14},{10,12},{12,10},{14,8},{16,22},{18,... | collective-permute-start | bytes 786440 | tf_op jit(solution)/shard_map/ppermute | solution.py:280
  28.7 8.5 %collective-permute-start.4 = (bf16[1024,128]{1,0:T(8,128)(2,1)S(1)}, bf16[1024,128]{1,0:T(8,128)(2,1)S(1)}, u32[]{:S(2)}, u32[]{:S(2)}) collective-permute-start(bf16[1024,128]{1,0:T(8,128)(2,1)S(1)} %get-tuple-element.58), channel_id=1, source_target_pairs={{0,4},{2,6},{4,0},{6,2},{8,12},{10,14},{12,8},{14,10},{16,20},{18,... | collective-permute-start | bytes 786440 | tf_op jit(solution)/shard_map/ppermute | solution.py:280
  30.7 8.0 %collective-permute-start.3 = (bf16[1024,128]{1,0:T(8,128)(2,1)S(1)}, bf16[1024,128]{1,0:T(8,128)(2,1)S(1)}, u32[]{:S(2)}, u32[]{:S(2)}) collective-permute-start(bf16[1024,128]{1,0:T(8,128)(2,1)S(1)} %get-tuple-element.59), channel_id=1, source_target_pairs={{0,2},{2,0},{4,6},{6,4},{8,10},{10,8},{12,14},{14,12},{16,18},{18,... | collective-permute-start | bytes 786440 | tf_op jit(solution)/shard_map/ppermute | solution.py:280
  31.7 11.1 %collective-permute-start.11 = (bf16[128,1024]{1,0:T(8,128)(2,1)S(1)}, bf16[128,1024]{1,0:T(8,128)(2,1)S(1)}, u32[]{:S(2)}, u32[]{:S(2)}) collective-permute-start(bf16[128,1024]{1,0:T(8,128)(2,1)S(1)} %pad_maximum_fusion.2.refs_0_), channel_id=1, source_target_pairs={{0,24},{2,26},{4,28},{6,30},{8,16},{10,18},{12,20},{14,22},{16,8},... | collective-permute-start | bytes 786440 | tf_op jit(solution)/shard_map/ppermute | solution.py:280
  35.3 21.9 %collective-permute-start.10 = (bf16[128,1024]{1,0:T(8,128)(2,1)S(1)}, bf16[128,1024]{1,0:T(8,128)(2,1)S(1)}, u32[]{:S(2)}, u32[]{:S(2)}) collective-permute-start(bf16[128,1024]{1,0:T(8,128)(2,1)S(1)} %pad_maximum_fusion.2.refs_0_), channel_id=1, source_target_pairs={{0,16},{2,18},{4,20},{6,22},{8,24},{10,26},{12,28},{14,30},{16,0},... | collective-permute-start | bytes 786440 | tf_op jit(solution)/shard_map/ppermute | solution.py:280
  36.4 20.8 %collective-permute-start.9 = (bf16[128,1024]{1,0:T(8,128)(2,1)S(1)}, bf16[128,1024]{1,0:T(8,128)(2,1)S(1)}, u32[]{:S(2)}, u32[]{:S(2)}) collective-permute-start(bf16[128,1024]{1,0:T(8,128)(2,1)S(1)} %pad_maximum_fusion.2.refs_0_), channel_id=1, source_target_pairs={{0,8},{2,10},{4,12},{6,14},{8,0},{10,2},{12,4},{14,6},{16,24},{18,... | collective-permute-start | bytes 786440 | tf_op jit(solution)/shard_map/ppermute | solution.py:280
  75.4 18.1 %collective-permute-start.12 = (bf16[128,1152]{1,0:T(8,128)(2,1)S(1)}, bf16[128,1152]{1,0:T(8,128)(2,1)S(1)}, u32[]{:S(2)}, u32[]{:S(2)}) collective-permute-start(bf16[128,1152]{1,0:T(8,128)(2,1)S(1)} %block_attention.6), channel_id=1, source_target_pairs={{0,8},{2,10},{4,12},{6,14},{8,0},{10,2},{12,4},{14,6},{16,24},{18,... | collective-permute-start | bytes 884744 | tf_op jit(solution)/shard_map/ppermute | solution.py:280
  75.7 70.6 %collective-permute-start.20 = (bf16[1024,512]{1,0:T(8,128)(2,1)S(1)}, bf16[1024,512]{1,0:T(8,128)(2,1)S(1)}, u32[]{:S(2)}, u32[]{:S(2)}) collective-permute-start(bf16[1024,512]{1,0:T(8,128)(2,1)S(1)} %get-tuple-element.49), channel_id=1, source_target_pairs={{0,6},{2,4},{4,2},{6,0},{8,14},{10,12},{12,10},{14,8},{16,22},{18,... | collective-permute-start | bytes 3145736 | tf_op jit(solution)/shard_map/ppermute | solution.py:280
  79.0 67.3 %collective-permute-start.19 = (bf16[1024,512]{1,0:T(8,128)(2,1)S(1)}, bf16[1024,512]{1,0:T(8,128)(2,1)S(1)}, u32[]{:S(2)}, u32[]{:S(2)}) collective-permute-start(bf16[1024,512]{1,0:T(8,128)(2,1)S(1)} %get-tuple-element.50), channel_id=1, source_target_pairs={{0,4},{2,6},{4,0},{6,2},{8,12},{10,14},{12,8},{14,10},{16,20},{18,... | collective-permute-start | bytes 3145736 | tf_op jit(solution)/shard_map/ppermute | solution.py:280
  79.0 67.3 %collective-permute-start.18 = (bf16[1024,512]{1,0:T(8,128)(2,1)S(1)}, bf16[1024,512]{1,0:T(8,128)(2,1)S(1)}, u32[]{:S(2)}, u32[]{:S(2)}) collective-permute-start(bf16[1024,512]{1,0:T(8,128)(2,1)S(1)} %get-tuple-element.51), channel_id=1, source_target_pairs={{0,2},{2,0},{4,6},{6,4},{8,10},{10,8},{12,14},{14,12},{16,18},{18,... | collective-permute-start | bytes 3145736 | tf_op jit(solution)/shard_map/ppermute | solution.py:280
  79.7 32.5 %collective-permute-start.13 = (bf16[128,1152]{1,0:T(8,128)(2,1)S(1)}, bf16[128,1152]{1,0:T(8,128)(2,1)S(1)}, u32[]{:S(2)}, u32[]{:S(2)}) collective-permute-start(bf16[128,1152]{1,0:T(8,128)(2,1)S(1)} %block_attention.5), channel_id=1, source_target_pairs={{0,16},{2,18},{4,20},{6,22},{8,24},{10,26},{12,28},{14,30},{16,0},... | collective-permute-start | bytes 884744 | tf_op jit(solution)/shard_map/ppermute | solution.py:280
  93.5 18.7 %collective-permute-start.14 = (bf16[128,1152]{1,0:T(8,128)(2,1)S(1)}, bf16[128,1152]{1,0:T(8,128)(2,1)S(1)}, u32[]{:S(2)}, u32[]{:S(2)}) collective-permute-start(bf16[128,1152]{1,0:T(8,128)(2,1)S(1)} %block_attention.4), channel_id=1, source_target_pairs={{0,24},{2,26},{4,28},{6,30},{8,16},{10,18},{12,20},{14,22},{16,8},... | collective-permute-start | bytes 884744 | tf_op jit(solution)/shard_map/ppermute | solution.py:280
  113.0 12.7 %collective-permute-start.17 = (bf16[128,1024]{1,0:T(8,128)(2,1)S(1)}, bf16[128,1024]{1,0:T(8,128)(2,1)S(1)}, u32[]{:S(2)}, u32[]{:S(2)}) collective-permute-start(bf16[128,1024]{1,0:T(8,128)(2,1)S(1)} %combine.1.refs_0_), channel_id=1, source_target_pairs={{0,24},{2,26},{4,28},{6,30},{8,16},{10,18},{12,20},{14,22},{16,8},... | collective-permute-start | bytes 786440 | tf_op jit(solution)/shard_map/ppermute | solution.py:280
  115.4 26.7 %collective-permute-start.16 = (bf16[128,1024]{1,0:T(8,128)(2,1)S(1)}, bf16[128,1024]{1,0:T(8,128)(2,1)S(1)}, u32[]{:S(2)}, u32[]{:S(2)}) collective-permute-start(bf16[128,1024]{1,0:T(8,128)(2,1)S(1)} %combine.1.refs_0_), channel_id=1, source_target_pairs={{0,16},{2,18},{4,20},{6,22},{8,24},{10,26},{12,28},{14,30},{16,0},... | collective-permute-start | bytes 786440 | tf_op jit(solution)/shard_map/ppermute | solution.py:280
  125.8 20.6 %collective-permute-start.15 = (bf16[128,1024]{1,0:T(8,128)(2,1)S(1)}, bf16[128,1024]{1,0:T(8,128)(2,1)S(1)}, u32[]{:S(2)}, u32[]{:S(2)}) collective-permute-start(bf16[128,1024]{1,0:T(8,128)(2,1)S(1)} %combine.1.refs_0_), channel_id=1, source_target_pairs={{0,8},{2,10},{4,12},{6,14},{8,0},{10,2},{12,4},{14,6},{16,24},{18,... | collective-permute-start | bytes 786440 | tf_op jit(solution)/shard_map/ppermute | solution.py:280
  152.7 9.2 %collective-permute-start.22 = (bf16[256,512]{1,0:T(8,128)(2,1)S(1)}, bf16[256,512]{1,0:T(8,128)(2,1)S(1)}, u32[]{:S(2)}, u32[]{:S(2)}) collective-permute-start(bf16[256,512]{1,0:T(8,128)(2,1)S(1)} %get-tuple-element.53), channel_id=1, source_target_pairs={{0,2},{2,0},{4,6},{6,4},{8,10},{10,8},{12,14},{14,12},{16,18},{18,... | collective-permute-start | bytes 786440 | tf_op jit(solution)/shard_map/ppermute | solution.py:280
  154.2 13.4 %collective-permute-start.24 = (bf16[256,512]{1,0:T(8,128)(2,1)S(1)}, bf16[256,512]{1,0:T(8,128)(2,1)S(1)}, u32[]{:S(2)}, u32[]{:S(2)}) collective-permute-start(bf16[256,512]{1,0:T(8,128)(2,1)S(1)} %get-tuple-element.54), channel_id=1, source_target_pairs={{0,6},{2,4},{4,2},{6,0},{8,14},{10,12},{12,10},{14,8},{16,22},{18,... | collective-permute-start | bytes 786440 | tf_op jit(solution)/shard_map/ppermute | solution.py:280
  155.6 13.5 %collective-permute-start.23 = (bf16[256,512]{1,0:T(8,128)(2,1)S(1)}, bf16[256,512]{1,0:T(8,128)(2,1)S(1)}, u32[]{:S(2)}, u32[]{:S(2)}) collective-permute-start(bf16[256,512]{1,0:T(8,128)(2,1)S(1)} %get-tuple-element.55), channel_id=1, source_target_pairs={{0,4},{2,6},{4,0},{6,2},{8,12},{10,14},{12,8},{14,10},{16,20},{18,... | collective-permute-start | bytes 786440 | tf_op jit(solution)/shard_map/ppermute | solution.py:280
  (7 other events, 44.3 us)
where the time goes:
time: 170 us
  starting transfers between devices  67.7 us (40%)
  waiting for transfers between devices  61.5 us (36%)
  Pallas kernels  28 us (16%)
  other arithmetic  7.55 us (4%)
  local copies, waits for them, and re-layouts  4.86 us (3%)
    ppermute x24, starting transfers between devices, swap(): lax.ppermute(x, 'ctx', [(i, i ^ mask) for i in range(ctx_count)])  67.6 us
    ppermute x24, waiting for transfers between devices, swap(): lax.ppermute(x, 'ctx', [(i, i ^ mask) for i in range(ctx_count)])  58.9 us
    pallas_call x4, Pallas kernels, block_attention(): pl.pallas_call(partial(attention_kernel, scale2=float(width) ** (-0.5) *...  24.1 us
  transfers between devices with their start and end apart: 25, of which 11 were waited for; matrix products, arithmetic and copies ran while one was open for 5% of the time, Pallas kernels for 4%

commit v1 on v0

--- a/solution.py
+++ b/solution.py
@@ -19,7 +19,7 @@
 def attention_kernel(
     turn_ref, count_ref, diag_ref, klist_ref, slist_ref, table_ref, k_ref, v_ref, *refs, scale2, list_len, pieces,
 ):
-    *q_refs, o_ref, q_ref, even_sc, odd_sc, diag_sc = refs
+    *q_refs, o_ref, q_ref, even_sc, odd_sc, diag_sc, m_sc, total_sc, acc_sc = refs
     width = k_ref.shape[1]
     heads = q_ref.shape[1] // width
     turn = turn_ref[0]
@@ -60,7 +60,6 @@
     def _():
         diag_sc[...] = jnp.full(diag_sc.shape, NEG_FILL, jnp.float32)
 
-    diag_values = block_of(v_ref, jnp.maximum(diag, 0))
     counts = [count_ref[turn * heads + h] for h in range(heads)]
     chunks = [(c + CHUNK - 1) // CHUNK for c in counts]
 
@@ -91,14 +90,10 @@
         return top
 
     top = lax.fori_loop(0, chunks[0], first, top_start)
-    lane = lax.broadcasted_iota(jnp.int32, (BLOCK, BLOCK), 1)
-    lse = jnp.full((BLOCK, BLOCK), NEG_FILL, jnp.float32)
+    zeros = jnp.zeros((BLOCK, BLOCK), jnp.float32)
     for h in range(heads):
         top = jnp.maximum(jnp.where(counts[h] > 0, top, NEG_FILL), diag_sc[h])
         m = jnp.max(top, axis=1, keepdims=True)
-        total = jnp.exp2(diag_sc[h] - m)
-        total = jnp.where(diag >= 0, total, 0.0)
-        acc = jnp.dot(total.astype(jnp.bfloat16), diag_values, preferred_element_type=jnp.float32)
         if h + 1 < heads:
 
             def both(t, carry, h=h, m=m):
@@ -109,7 +104,7 @@
                 return top, total, acc
 
             top, total, acc = lax.fori_loop(
-                0, jnp.maximum(chunks[h], chunks[h + 1]), both, (top_start, total, acc)
+                0, jnp.maximum(chunks[h], chunks[h + 1]), both, (top_start, zeros, zeros)
             )
         else:
 
@@ -118,13 +113,28 @@
                     carry = value_part(h, t, u, m, *carry)
                 return carry
 
-            total, acc = lax.fori_loop(0, chunks[h], last, (total, acc))
-        total = jnp.sum(total, axis=1, keepdims=True)
+            total, acc = lax.fori_loop(0, chunks[h], last, (zeros, zeros))
+        m_sc[h] = jnp.broadcast_to(m, (BLOCK, BLOCK))
+        total_sc[h] = total
+        acc_sc[h] = acc
+
+    @pl.when(diag >= 0)
+    def _():
+        values = block_of(v_ref, diag)
+        for h in range(heads):
+            p = jnp.exp2(diag_sc[h] - m_sc[h])
+            total_sc[h] += p
+            acc_sc[h] += jnp.dot(p.astype(jnp.bfloat16), values, preferred_element_type=jnp.float32)
+
+    lane = lax.broadcasted_iota(jnp.int32, (BLOCK, BLOCK), 1)
+    lse = jnp.full((BLOCK, BLOCK), NEG_FILL, jnp.float32)
+    for h in range(heads):
+        total = jnp.sum(total_sc[h], axis=1, keepdims=True)
         seen = total > 0.0
         safe = jnp.where(seen, total, 1.0)
-        o_ref[:, h * width : (h + 1) * width] = (acc / safe).astype(o_ref.dtype)
+        o_ref[:, h * width : (h + 1) * width] = (acc_sc[h] * (1.0 / safe)).astype(o_ref.dtype)
         mine = (lane == h) | (lane == heads + h) | (lane == 2 * heads + h)
-        lse = jnp.where(mine & seen, m + jnp.log2(safe), lse)
+        lse = jnp.where(mine & seen, m_sc[h] + jnp.log2(safe), lse)
     high = lse.astype(jnp.bfloat16)
     rest = lse - high.astype(jnp.float32)
     middle = rest.astype(jnp.bfloat16)
@@ -155,8 +165,8 @@
             pltpu.VMEM((BLOCK, heads * width), jnp.bfloat16),
             pltpu.VMEM((list_len + 1, BLOCK, BLOCK), jnp.float32),
             pltpu.VMEM((list_len + 1, BLOCK, BLOCK), jnp.float32),
-            pltpu.VMEM((heads, BLOCK, BLOCK), jnp.float32),
-        ],
+        ]
+        + [pltpu.VMEM((heads, BLOCK, BLOCK), jnp.float32)] * 4,
         compiler_params=pltpu.CompilerParams(vmem_limit_bytes=VMEM_LIMIT),
         name="block_attention",
     )(jnp.full((1,), turn, jnp.int32), count, diag, klist, slist, table, keys, values, *q_parts)
@@ -315,14 +325,15 @@
         ),
     )
     source = (turns[:, None] * plane + jnp.arange(plane, dtype=jnp.int32)[None, :]) ^ place
-    table = (line_of(source) * plane + plane_of(source)).reshape(-1)
+    table = plane_of(source).reshape(-1)
     share = lines // core_count
     steps = jnp.arange(core_count, dtype=jnp.int32)
     half = jnp.where(core + steps >= core_count, core + steps - core_count, core + steps)
     order = (half[:, None] * share + jnp.arange(share, dtype=jnp.int32)[None, :]).reshape(-1) ^ line
 
-    keys, values, weight, table, order, meta, q_parts = lax.optimization_barrier(
-        (keys, values, out_weight, table, order, meta, q_parts)
+    visits = ([2, 3, 1] + list(range(4, lines)) if lines >= 4 else list(range(1, lines))) + [0]
+    keys, values, weight, table, order, meta, q_parts[visits[0]] = lax.optimization_barrier(
+        (keys, values, out_weight, table, order, meta, q_parts[visits[0]])
     )
     slabs = [lax.dynamic_slice_in_dim(weight, (mine ^ m) * feats, feats, 0) for m in range(plane)]
     weights = []
@@ -330,8 +341,8 @@
         weights.append(swap(slabs[m], m))
 
     outs = [None] * lines
-    for k in reversed(range(lines)):
-        o = block_attention(k, meta, table, q_parts, keys, values)
+    for k in visits:
+        o = block_attention(k, meta, table, [q_parts[k]], keys, values)
         if k:
             keys, o = lax.optimization_barrier((keys, o))
         outs[k] = swap(o, line_mask(k))

time: 170 us -> 170 us (level)
  waiting for transfers between devices: 61.5 us -> 80.3 us
  starting transfers between devices: 67.7 us -> 51.8 us
  Pallas kernels: 28 us -> 24.7 us
    ppermute x24, waiting for transfers between devices: 58.9 us -> 77.7 us  [swap(): lax.ppermute(x, 'ctx', [(i, i ^ mask) for i in range(ctx_count)])]
    ppermute x24, starting transfers between devices: 67.6 us -> 51.7 us  [swap(): lax.ppermute(x, 'ctx', [(i, i ^ mask) for i in range(ctx_count)])]
    pallas_call x4, Pallas kernels: 24.1 us -> 20.8 us  [block_attention(): pl.pallas_call(partial(attention_kernel, scale2=float(width) ** (-0.5) *...]
  transfers between devices with their start and end apart: 25 -> 25, of which waited for: 11 -> 12; matrix products, arithmetic and copies ran while one was open for 5% -> 5% of each run, Pallas kernels for 4% -> 10%
where the time goes in v1:
time: 170 us; the launch traced here: 169 us
  waiting for transfers between devices  80.3 us (47%)
  starting transfers between devices  51.8 us (30%)
  Pallas kernels  24.7 us (15%)
  other arithmetic  7.55 us (4%)
  local copies, waits for them, and re-layouts  4.86 us (3%)
    ppermute x24, waiting for transfers between devices, swap(): lax.ppermute(x, 'ctx', [(i, i ^ mask) for i in range(ctx_count)])  77.7 us
    ppermute x24, starting transfers between devices, swap(): lax.ppermute(x, 'ctx', [(i, i ^ mask) for i in range(ctx_count)])  51.7 us
    pallas_call x4, Pallas kernels, block_attention(): pl.pallas_call(partial(attention_kernel, scale2=float(width) ** (-0.5) *...  20.8 us
  transfers between devices with their start and end apart: 25, of which 12 were waited for; matrix products, arithmetic and copies ran while one was open for 5% of the time, Pallas kernels for 10%

profile of v1, /device:TPU:0, one launch (start us, length us, event | category | flops | bytes accessed | tf_op | source)
XLA Modules:
  0.0 169.5 jit_solution(2564089213993793178)
XLA Ops:
  0.0 1.6 constant_dynamic-slice_fusion.7
  1.6 3.0 %collective-permute-start.6 = (bf16[32,1024]{1,0:T(8,128)(2,1)}, bf16[32,1024]{1,0:T(8,128)(2,1)}, u32[]{:S(2)}, u32[]{:S(2)}) collective-permute-start(bf16[32,1024]{1,0:T(8,128)(2,1)} %get-tuple-element.59), channel_id=1, source_target_pairs={{0,2},{2,0},{4,6},{6,4},{8,10},{10,8},{12,14},{14,12},{16,18},{18,... | collective-permute-start | bytes 196616 | tf_op jit(solution)/shard_map/ppermute | solution.py:290
  17.0 2.9 %collective-permute-start.5 = (bf16[1024,128]{1,0:T(8,128)(2,1)S(1)}, bf16[1024,128]{1,0:T(8,128)(2,1)S(1)}, u32[]{:S(2)}, u32[]{:S(2)}) collective-permute-start(bf16[1024,128]{1,0:T(8,128)(2,1)S(1)} %get-tuple-element.51), channel_id=1, source_target_pairs={{0,6},{2,4},{4,2},{6,0},{8,14},{10,12},{12,10},{14,8},{16,22},{18,... | collective-permute-start | bytes 786440 | tf_op jit(solution)/shard_map/ppermute | solution.py:290
  19.9 8.9 %collective-permute-done.7 = bf16[32,1024]{1,0:T(8,128)(2,1)S(1)} collective-permute-done((bf16[32,1024]{1,0:T(8,128)(2,1)}, bf16[32,1024]{1,0:T(8,128)(2,1)S(1)}, u32[]{:S(2)}, u32[]{:S(2)}) %collective-permute-start.7) | collective-permute-done | bytes 65568 | tf_op jit(solution)/shard_map/ppermute | solution.py:290
  33.3 2.5 %collective-permute-start.10 = (bf16[128,1024]{1,0:T(8,128)(2,1)S(1)}, bf16[128,1024]{1,0:T(8,128)(2,1)S(1)}, u32[]{:S(2)}, u32[]{:S(2)}) collective-permute-start(bf16[128,1024]{1,0:T(8,128)(2,1)S(1)} %pad_maximum_fusion.2.refs_0_), channel_id=1, source_target_pairs={{0,24},{2,26},{4,28},{6,30},{8,16},{10,18},{12,20},{14,22},{16,8},... | collective-permute-start | bytes 786440 | tf_op jit(solution)/shard_map/ppermute | solution.py:290
  37.1 1.6 collective-permute-done.3
  38.7 19.6 %collective-permute-done.9.refs_0_ = bf16[128,1024]{1,0:T(8,128)(2,1)S(1)} collective-permute-done((bf16[128,1024]{1,0:T(8,128)(2,1)S(1)}, bf16[128,1024]{1,0:T(8,128)(2,1)S(1)}, u32[]{:S(2)}, u32[]{:S(2)}) %collective-permute-start.9) | collective-permute-done | bytes 262176 | tf_op jit(solution)/shard_map/ppermute | solution.py:290
  58.4 5.1 %block_attention.4 = bf16[128,1152]{1,0:T(8,128)(2,1)S(1)} custom-call(s32[1]{0:T(128)} %constant.63.clone.1.turn_ref, s32[32]{0:T(128)S(1)} %reshape.120.count_ref, s32[4]{0:T(128)S(1)} %broadcast_select_fusion.diag_ref, s32[1024]{0:T(1024)S(1)} %reshape.121.klist_ref, s32[1024]{0:T(1024)S(1)} %compare_select_fusion.slist_ref, s32[16]{0:T(128)S(1)} %and.26.table_ref, ...), custom_call_target="tpu_custom_call" | custom-call | tf_op jit(solution)/shard_map/block_attention/pallas_call | solution.py:154
  63.5 5.1 %block_attention.5 = bf16[128,1152]{1,0:T(8,128)(2,1)S(1)} custom-call(s32[1]{0:T(128)} %constant.64.clone.1.turn_ref, s32[32]{0:T(128)S(1)} %reshape.120.count_ref, s32[4]{0:T(128)S(1)} %broadcast_select_fusion.diag_ref, s32[1024]{0:T(1024)S(1)} %reshape.121.klist_ref, s32[1024]{0:T(1024)S(1)} %compare_select_fusion.slist_ref, s32[16]{0:T(128)S(1)} %and.26.table_ref, ...), custom_call_target="tpu_custom_call" | custom-call | tf_op jit(solution)/shard_map/block_attention/pallas_call | solution.py:154
  68.7 5.4 %block_attention.6 = bf16[128,1152]{1,0:T(8,128)(2,1)S(1)} custom-call(s32[1]{0:T(128)} %constant.65.clone.1.turn_ref, s32[32]{0:T(128)S(1)} %reshape.120.count_ref, s32[4]{0:T(128)S(1)} %broadcast_select_fusion.diag_ref, s32[1024]{0:T(1024)S(1)} %reshape.121.klist_ref, s32[1024]{0:T(1024)S(1)} %compare_select_fusion.slist_ref, s32[16]{0:T(128)S(1)} %and.26.table_ref, ...), custom_call_target="tpu_custom_call" | custom-call | tf_op jit(solution)/shard_map/block_attention/pallas_call | solution.py:154
  74.4 3.3 %collective-permute-start.20 = (bf16[1024,512]{1,0:T(8,128)(2,1)S(1)}, bf16[1024,512]{1,0:T(8,128)(2,1)S(1)}, u32[]{:S(2)}, u32[]{:S(2)}) collective-permute-start(bf16[1024,512]{1,0:T(8,128)(2,1)S(1)} %get-tuple-element.43), channel_id=1, source_target_pairs={{0,6},{2,4},{4,2},{6,0},{8,14},{10,12},{12,10},{14,8},{16,22},{18,... | collective-permute-start | bytes 3145736 | tf_op jit(solution)/shard_map/ppermute | solution.py:290
  78.3 14.1 %collective-permute-start.14 = (bf16[128,1152]{1,0:T(8,128)(2,1)S(1)}, bf16[128,1152]{1,0:T(8,128)(2,1)S(1)}, u32[]{:S(2)}, u32[]{:S(2)}) collective-permute-start(bf16[128,1152]{1,0:T(8,128)(2,1)S(1)} %block_attention.5), channel_id=1, source_target_pairs={{0,24},{2,26},{4,28},{6,30},{8,16},{10,18},{12,20},{14,22},{16,8},... | collective-permute-start | bytes 884744 | tf_op jit(solution)/shard_map/ppermute | solution.py:290
  93.2 5.2 %block_attention.7.refs_0_ = bf16[128,1152]{1,0:T(8,128)(2,1)S(1)} custom-call(s32[1]{0:T(128)} %constant.62.clone.1.turn_ref, s32[32]{0:T(128)S(1)} %reshape.120.count_ref, s32[4]{0:T(128)S(1)} %broadcast_select_fusion.diag_ref, s32[1024]{0:T(1024)S(1)} %reshape.121.klist_ref, s32[1024]{0:T(1024)S(1)} %compare_select_fusion.slist_ref, ...), custom_call_target="tpu_custom_call" | custom-call | tf_op jit(solution)/shard_map/block_attention/pallas_call | solution.py:154
  98.4 2.0 %collective-permute-done.14.refs_3_ = bf16[128,1152]{1,0:T(8,128)(2,1)S(1)} collective-permute-done((bf16[128,1152]{1,0:T(8,128)(2,1)S(1)}, bf16[128,1152]{1,0:T(8,128)(2,1)S(1)}, u32[]{:S(2)}, u32[]{:S(2)}) %collective-permute-start.14) | collective-permute-done | bytes 294944 | tf_op jit(solution)/shard_map/ppermute | solution.py:290
  100.4 16.1 %collective-permute-done.13.refs_2_ = bf16[128,1152]{1,0:T(8,128)(2,1)S(1)} collective-permute-done((bf16[128,1152]{1,0:T(8,128)(2,1)S(1)}, bf16[128,1152]{1,0:T(8,128)(2,1)S(1)}, u32[]{:S(2)}, u32[]{:S(2)}) %collective-permute-start.13) | collective-permute-done | bytes 294944 | tf_op jit(solution)/shard_map/ppermute | solution.py:290
  117.3 2.7 %collective-permute-start.17 = (bf16[128,1024]{1,0:T(8,128)(2,1)S(1)}, bf16[128,1024]{1,0:T(8,128)(2,1)S(1)}, u32[]{:S(2)}, u32[]{:S(2)}) collective-permute-start(bf16[128,1024]{1,0:T(8,128)(2,1)S(1)} %combine.1.refs_0_), channel_id=1, source_target_pairs={{0,24},{2,26},{4,28},{6,30},{8,16},{10,18},{12,20},{14,22},{16,8},... | collective-permute-start | bytes 786440 | tf_op jit(solution)/shard_map/ppermute | solution.py:290
  120.0 8.4 %collective-permute-done.17.refs_3_ = bf16[128,1024]{1,0:T(8,128)(2,1)S(1)} collective-permute-done((bf16[128,1024]{1,0:T(8,128)(2,1)S(1)}, bf16[128,1024]{1,0:T(8,128)(2,1)S(1)}, u32[]{:S(2)}, u32[]{:S(2)}) %collective-permute-start.17) | collective-permute-done | bytes 262176 | tf_op jit(solution)/shard_map/ppermute | solution.py:290
  128.4 9.2 %collective-permute-start.15 = (bf16[128,1024]{1,0:T(8,128)(2,1)S(1)}, bf16[128,1024]{1,0:T(8,128)(2,1)S(1)}, u32[]{:S(2)}, u32[]{:S(2)}) collective-permute-start(bf16[128,1024]{1,0:T(8,128)(2,1)S(1)} %combine.1.refs_0_), channel_id=1, source_target_pairs={{0,8},{2,10},{4,12},{6,14},{8,0},{10,2},{12,4},{14,6},{16,24},{18,... | collective-permute-start | bytes 786440 | tf_op jit(solution)/shard_map/ppermute | solution.py:290
  137.6 3.6 %collective-permute-done.16.refs_2_ = bf16[128,1024]{1,0:T(8,128)(2,1)S(1)} collective-permute-done((bf16[128,1024]{1,0:T(8,128)(2,1)S(1)}, bf16[128,1024]{1,0:T(8,128)(2,1)S(1)}, u32[]{:S(2)}, u32[]{:S(2)}) %collective-permute-start.16) | collective-permute-done | bytes 262176 | tf_op jit(solution)/shard_map/ppermute | solution.py:290
  141.2 4.7 %collective-permute-done.15.refs_1_ = bf16[128,1024]{1,0:T(8,128)(2,1)S(1)} collective-permute-done((bf16[128,1024]{1,0:T(8,128)(2,1)S(1)}, bf16[128,1024]{1,0:T(8,128)(2,1)S(1)}, u32[]{:S(2)}, u32[]{:S(2)}) %collective-permute-start.15) | collective-permute-done | bytes 262176 | tf_op jit(solution)/shard_map/ppermute | solution.py:290
  145.8 3.1 %project.1 = (bf16[4,1,256,512]{3,2,1,0:T(8,128)(2,1)S(1)}, f32[4,256,512]{2,1,0:T(8,128)S(1)}) custom-call(s32[4]{0:T(128)S(1)} %xor.66.order_ref, bf16[128,1024]{1,0:T(8,128)(2,1)S(1)} %combine.1.refs_0_, bf16[128,1024]{1,0:T(8,128)(2,1)S(1)} %collective-permute-done.15.refs_1_, bf16[128,1024]{1,0:T(8,128)(2,1)S(1)} %collective-permute-done.16.refs_2_, ...), custom_call_target="tpu_custom_call" | custom-call | tf_op jit(solution)/shard_map/project/pallas_call | solution.py:231
  149.0 2.6 %collective-permute-done.21 = bf16[4,256,512]{2,1,0:T(8,128)(2,1)S(1)} collective-permute-done((bf16[4,256,512]{2,1,0:T(8,128)(2,1)S(1)}, bf16[4,256,512]{2,1,0:T(8,128)(2,1)S(1)}, u32[]{:S(2)}, u32[]{:S(2)}) %collective-permute-start.21) | collective-permute-done | bytes 1048608 | tf_op jit(solution)/shard_map/ppermute | solution.py:354
  155.8 5.7 %collective-permute-done.22 = bf16[256,512]{1,0:T(8,128)(2,1)S(1)} collective-permute-done((bf16[256,512]{1,0:T(8,128)(2,1)S(1)}, bf16[256,512]{1,0:T(8,128)(2,1)S(1)}, u32[]{:S(2)}, u32[]{:S(2)}) %collective-permute-start.22) | collective-permute-done | bytes 262176 | tf_op jit(solution)/shard_map/ppermute | solution.py:290
  161.5 5.7 %collective-permute-done.24 = bf16[256,512]{1,0:T(8,128)(2,1)S(1)} collective-permute-done((bf16[256,512]{1,0:T(8,128)(2,1)S(1)}, bf16[256,512]{1,0:T(8,128)(2,1)S(1)}, u32[]{:S(2)}, u32[]{:S(2)}) %collective-permute-start.24) | collective-permute-done | bytes 262176 | tf_op jit(solution)/shard_map/ppermute | solution.py:290
  (86 shorter events, 27.2 us)
Async XLA Ops:
  1.6 14.1 %collective-permute-start.6 = (bf16[32,1024]{1,0:T(8,128)(2,1)}, bf16[32,1024]{1,0:T(8,128)(2,1)}, u32[]{:S(2)}, u32[]{:S(2)}) collective-permute-start(bf16[32,1024]{1,0:T(8,128)(2,1)} %get-tuple-element.59), channel_id=1, source_target_pairs={{0,2},{2,0},{4,6},{6,4},{8,10},{10,8},{12,14},{14,12},{16,18},{18,... | collective-permute-start | bytes 196616 | tf_op jit(solution)/shard_map/ppermute | solution.py:290
  4.6 12.4 %collective-permute-start.8 = (bf16[32,1024]{1,0:T(8,128)(2,1)}, bf16[32,1024]{1,0:T(8,128)(2,1)}, u32[]{:S(2)}, u32[]{:S(2)}) collective-permute-start(bf16[32,1024]{1,0:T(8,128)(2,1)} %get-tuple-element.60), channel_id=1, source_target_pairs={{0,6},{2,4},{4,2},{6,0},{8,14},{10,12},{12,10},{14,8},{16,22},{18,... | collective-permute-start | bytes 196616 | tf_op jit(solution)/shard_map/ppermute | solution.py:290
  7.7 23.0 %collective-permute-start.2 = (bf16[1024,128]{1,0:T(8,128)(2,1)S(1)}, bf16[1024,128]{1,0:T(8,128)(2,1)S(1)}, u32[]{:S(2)}, u32[]{:S(2)}) collective-permute-start(bf16[1024,128]{1,0:T(8,128)(2,1)S(1)} %get-tuple-element.55), channel_id=1, source_target_pairs={{0,6},{2,4},{4,2},{6,0},{8,14},{10,12},{12,10},{14,8},{16,22},{18,... | collective-permute-start | bytes 786440 | tf_op jit(solution)/shard_map/ppermute | solution.py:290
  9.2 22.6 %collective-permute-start.1 = (bf16[1024,128]{1,0:T(8,128)(2,1)S(1)}, bf16[1024,128]{1,0:T(8,128)(2,1)}, u32[]{:S(2)}, u32[]{:S(2)}) collective-permute-start(bf16[1024,128]{1,0:T(8,128)(2,1)S(1)} %get-tuple-element.56), channel_id=1, source_target_pairs={{0,4},{2,6},{4,0},{6,2},{8,12},{10,14},{12,8},{14,10},{16,20},{18,... | collective-permute-start | bytes 786440 | tf_op jit(solution)/shard_map/ppermute | solution.py:290
  10.7 22.6 %collective-permute-start = (bf16[1024,128]{1,0:T(8,128)(2,1)S(1)}, bf16[1024,128]{1,0:T(8,128)(2,1)}, u32[]{:S(2)}, u32[]{:S(2)}) collective-permute-start(bf16[1024,128]{1,0:T(8,128)(2,1)S(1)} %get-tuple-element.57), channel_id=1, source_target_pairs={{0,2},{2,0},{4,6},{6,4},{8,10},{10,8},{12,14},{14,12},{16,18},{18,... | collective-permute-start | bytes 786440 | tf_op jit(solution)/shard_map/ppermute | solution.py:290
  15.7 13.0 %collective-permute-start.7 = (bf16[32,1024]{1,0:T(8,128)(2,1)}, bf16[32,1024]{1,0:T(8,128)(2,1)S(1)}, u32[]{:S(2)}, u32[]{:S(2)}) collective-permute-start(bf16[32,1024]{1,0:T(8,128)(2,1)} %get-tuple-element.61), channel_id=1, source_target_pairs={{0,4},{2,6},{4,0},{6,2},{8,12},{10,14},{12,8},{14,10},{16,20},{18,... | collective-permute-start | bytes 196616 | tf_op jit(solution)/shard_map/ppermute | solution.py:290
  17.0 19.9 %collective-permute-start.5 = (bf16[1024,128]{1,0:T(8,128)(2,1)S(1)}, bf16[1024,128]{1,0:T(8,128)(2,1)S(1)}, u32[]{:S(2)}, u32[]{:S(2)}) collective-permute-start(bf16[1024,128]{1,0:T(8,128)(2,1)S(1)} %get-tuple-element.51), channel_id=1, source_target_pairs={{0,6},{2,4},{4,2},{6,0},{8,14},{10,12},{12,10},{14,8},{16,22},{18,... | collective-permute-start | bytes 786440 | tf_op jit(solution)/shard_map/ppermute | solution.py:290
  28.7 8.3 %collective-permute-start.4 = (bf16[1024,128]{1,0:T(8,128)(2,1)S(1)}, bf16[1024,128]{1,0:T(8,128)(2,1)S(1)}, u32[]{:S(2)}, u32[]{:S(2)}) collective-permute-start(bf16[1024,128]{1,0:T(8,128)(2,1)S(1)} %get-tuple-element.52), channel_id=1, source_target_pairs={{0,4},{2,6},{4,0},{6,2},{8,12},{10,14},{12,8},{14,10},{16,20},{18,... | collective-permute-start | bytes 786440 | tf_op jit(solution)/shard_map/ppermute | solution.py:290
  30.7 8.0 %collective-permute-start.3 = (bf16[1024,128]{1,0:T(8,128)(2,1)S(1)}, bf16[1024,128]{1,0:T(8,128)(2,1)S(1)}, u32[]{:S(2)}, u32[]{:S(2)}) collective-permute-start(bf16[1024,128]{1,0:T(8,128)(2,1)S(1)} %get-tuple-element.53), channel_id=1, source_target_pairs={{0,2},{2,0},{4,6},{6,4},{8,10},{10,8},{12,14},{14,12},{16,18},{18,... | collective-permute-start | bytes 786440 | tf_op jit(solution)/shard_map/ppermute | solution.py:290
  31.7 36.9 %collective-permute-start.11 = (bf16[128,1024]{1,0:T(8,128)(2,1)S(1)}, bf16[128,1024]{1,0:T(8,128)(2,1)S(1)}, u32[]{:S(2)}, u32[]{:S(2)}) collective-permute-start(bf16[128,1024]{1,0:T(8,128)(2,1)S(1)} %pad_maximum_fusion.2.refs_0_), channel_id=1, source_target_pairs={{0,8},{2,10},{4,12},{6,14},{8,0},{10,2},{12,4},{14,6},{16,24},{18,... | collective-permute-start | bytes 786440 | tf_op jit(solution)/shard_map/ppermute | solution.py:290
  33.3 30.2 %collective-permute-start.10 = (bf16[128,1024]{1,0:T(8,128)(2,1)S(1)}, bf16[128,1024]{1,0:T(8,128)(2,1)S(1)}, u32[]{:S(2)}, u32[]{:S(2)}) collective-permute-start(bf16[128,1024]{1,0:T(8,128)(2,1)S(1)} %pad_maximum_fusion.2.refs_0_), channel_id=1, source_target_pairs={{0,24},{2,26},{4,28},{6,30},{8,16},{10,18},{12,20},{14,22},{16,8},... | collective-permute-start | bytes 786440 | tf_op jit(solution)/shard_map/ppermute | solution.py:290
  36.9 21.5 %collective-permute-start.9 = (bf16[128,1024]{1,0:T(8,128)(2,1)S(1)}, bf16[128,1024]{1,0:T(8,128)(2,1)S(1)}, u32[]{:S(2)}, u32[]{:S(2)}) collective-permute-start(bf16[128,1024]{1,0:T(8,128)(2,1)S(1)} %pad_maximum_fusion.2.refs_0_), channel_id=1, source_target_pairs={{0,16},{2,18},{4,20},{6,22},{8,24},{10,26},{12,28},{14,30},{16,0},... | collective-permute-start | bytes 786440 | tf_op jit(solution)/shard_map/ppermute | solution.py:290
  74.0 18.4 %collective-permute-start.12 = (bf16[128,1152]{1,0:T(8,128)(2,1)S(1)}, bf16[128,1152]{1,0:T(8,128)(2,1)S(1)}, u32[]{:S(2)}, u32[]{:S(2)}) collective-permute-start(bf16[128,1152]{1,0:T(8,128)(2,1)S(1)} %block_attention.6), channel_id=1, source_target_pairs={{0,8},{2,10},{4,12},{6,14},{8,0},{10,2},{12,4},{14,6},{16,24},{18,... | collective-permute-start | bytes 884744 | tf_op jit(solution)/shard_map/ppermute | solution.py:290
  74.4 71.4 %collective-permute-start.20 = (bf16[1024,512]{1,0:T(8,128)(2,1)S(1)}, bf16[1024,512]{1,0:T(8,128)(2,1)S(1)}, u32[]{:S(2)}, u32[]{:S(2)}) collective-permute-start(bf16[1024,512]{1,0:T(8,128)(2,1)S(1)} %get-tuple-element.43), channel_id=1, source_target_pairs={{0,6},{2,4},{4,2},{6,0},{8,14},{10,12},{12,10},{14,8},{16,22},{18,... | collective-permute-start | bytes 3145736 | tf_op jit(solution)/shard_map/ppermute | solution.py:290
  77.7 68.1 %collective-permute-start.19 = (bf16[1024,512]{1,0:T(8,128)(2,1)S(1)}, bf16[1024,512]{1,0:T(8,128)(2,1)S(1)}, u32[]{:S(2)}, u32[]{:S(2)}) collective-permute-start(bf16[1024,512]{1,0:T(8,128)(2,1)S(1)} %get-tuple-element.44), channel_id=1, source_target_pairs={{0,4},{2,6},{4,0},{6,2},{8,12},{10,14},{12,8},{14,10},{16,20},{18,... | collective-permute-start | bytes 3145736 | tf_op jit(solution)/shard_map/ppermute | solution.py:290
  77.7 68.1 %collective-permute-start.18 = (bf16[1024,512]{1,0:T(8,128)(2,1)S(1)}, bf16[1024,512]{1,0:T(8,128)(2,1)S(1)}, u32[]{:S(2)}, u32[]{:S(2)}) collective-permute-start(bf16[1024,512]{1,0:T(8,128)(2,1)S(1)} %get-tuple-element.45), channel_id=1, source_target_pairs={{0,2},{2,0},{4,6},{6,4},{8,10},{10,8},{12,14},{14,12},{16,18},{18,... | collective-permute-start | bytes 3145736 | tf_op jit(solution)/shard_map/ppermute | solution.py:290
  78.3 22.0 %collective-permute-start.14 = (bf16[128,1152]{1,0:T(8,128)(2,1)S(1)}, bf16[128,1152]{1,0:T(8,128)(2,1)S(1)}, u32[]{:S(2)}, u32[]{:S(2)}) collective-permute-start(bf16[128,1152]{1,0:T(8,128)(2,1)S(1)} %block_attention.5), channel_id=1, source_target_pairs={{0,24},{2,26},{4,28},{6,30},{8,16},{10,18},{12,20},{14,22},{16,8},... | collective-permute-start | bytes 884744 | tf_op jit(solution)/shard_map/ppermute | solution.py:290
  92.5 24.0 %collective-permute-start.13 = (bf16[128,1152]{1,0:T(8,128)(2,1)S(1)}, bf16[128,1152]{1,0:T(8,128)(2,1)S(1)}, u32[]{:S(2)}, u32[]{:S(2)}) collective-permute-start(bf16[128,1152]{1,0:T(8,128)(2,1)S(1)} %block_attention.4), channel_id=1, source_target_pairs={{0,16},{2,18},{4,20},{6,22},{8,24},{10,26},{12,28},{14,30},{16,0},... | collective-permute-start | bytes 884744 | tf_op jit(solution)/shard_map/ppermute | solution.py:290
  117.3 11.1 %collective-permute-start.17 = (bf16[128,1024]{1,0:T(8,128)(2,1)S(1)}, bf16[128,1024]{1,0:T(8,128)(2,1)S(1)}, u32[]{:S(2)}, u32[]{:S(2)}) collective-permute-start(bf16[128,1024]{1,0:T(8,128)(2,1)S(1)} %combine.1.refs_0_), channel_id=1, source_target_pairs={{0,24},{2,26},{4,28},{6,30},{8,16},{10,18},{12,20},{14,22},{16,8},... | collective-permute-start | bytes 786440 | tf_op jit(solution)/shard_map/ppermute | solution.py:290
  120.0 21.2 %collective-permute-start.16 = (bf16[128,1024]{1,0:T(8,128)(2,1)S(1)}, bf16[128,1024]{1,0:T(8,128)(2,1)S(1)}, u32[]{:S(2)}, u32[]{:S(2)}) collective-permute-start(bf16[128,1024]{1,0:T(8,128)(2,1)S(1)} %combine.1.refs_0_), channel_id=1, source_target_pairs={{0,16},{2,18},{4,20},{6,22},{8,24},{10,26},{12,28},{14,30},{16,0},... | collective-permute-start | bytes 786440 | tf_op jit(solution)/shard_map/ppermute | solution.py:290
  128.4 17.4 %collective-permute-start.15 = (bf16[128,1024]{1,0:T(8,128)(2,1)S(1)}, bf16[128,1024]{1,0:T(8,128)(2,1)S(1)}, u32[]{:S(2)}, u32[]{:S(2)}) collective-permute-start(bf16[128,1024]{1,0:T(8,128)(2,1)S(1)} %combine.1.refs_0_), channel_id=1, source_target_pairs={{0,8},{2,10},{4,12},{6,14},{8,0},{10,2},{12,4},{14,6},{16,24},{18,... | collective-permute-start | bytes 786440 | tf_op jit(solution)/shard_map/ppermute | solution.py:290
  152.2 9.2 %collective-permute-start.22 = (bf16[256,512]{1,0:T(8,128)(2,1)S(1)}, bf16[256,512]{1,0:T(8,128)(2,1)S(1)}, u32[]{:S(2)}, u32[]{:S(2)}) collective-permute-start(bf16[256,512]{1,0:T(8,128)(2,1)S(1)} %get-tuple-element.47), channel_id=1, source_target_pairs={{0,2},{2,0},{4,6},{6,4},{8,10},{10,8},{12,14},{14,12},{16,18},{18,... | collective-permute-start | bytes 786440 | tf_op jit(solution)/shard_map/ppermute | solution.py:290
  153.7 13.5 %collective-permute-start.24 = (bf16[256,512]{1,0:T(8,128)(2,1)S(1)}, bf16[256,512]{1,0:T(8,128)(2,1)S(1)}, u32[]{:S(2)}, u32[]{:S(2)}) collective-permute-start(bf16[256,512]{1,0:T(8,128)(2,1)S(1)} %get-tuple-element.48), channel_id=1, source_target_pairs={{0,6},{2,4},{4,2},{6,0},{8,14},{10,12},{12,10},{14,8},{16,22},{18,... | collective-permute-start | bytes 786440 | tf_op jit(solution)/shard_map/ppermute | solution.py:290
  155.1 13.5 %collective-permute-start.23 = (bf16[256,512]{1,0:T(8,128)(2,1)S(1)}, bf16[256,512]{1,0:T(8,128)(2,1)S(1)}, u32[]{:S(2)}, u32[]{:S(2)}) collective-permute-start(bf16[256,512]{1,0:T(8,128)(2,1)S(1)} %get-tuple-element.49), channel_id=1, source_target_pairs={{0,4},{2,6},{4,0},{6,2},{8,12},{10,14},{12,8},{14,10},{16,20},{18,... | collective-permute-start | bytes 786440 | tf_op jit(solution)/shard_map/ppermute | solution.py:290
  (7 other events, 42.7 us)

commit v2 on v1

--- a/solution.py
+++ b/solution.py
@@ -12,6 +12,7 @@
 BLOCK = 128
 NEG_FILL = -1e30
 CHUNK = 8
+HALF = 4
 STEP = 2
 VMEM_LIMIT = 20 << 20
 
@@ -61,20 +62,20 @@
         diag_sc[...] = jnp.full(diag_sc.shape, NEG_FILL, jnp.float32)
 
     counts = [count_ref[turn * heads + h] for h in range(heads)]
-    chunks = [(c + CHUNK - 1) // CHUNK for c in counts]
-
-    def score_part(h, t, u, top):
-        base = (turn * heads + h) * list_len + t * CHUNK + u
+    chunks = [(c + HALF - 1) // HALF for c in counts]
+
+    def score_part(h, slot, top):
+        base = (turn * heads + h) * list_len + slot
         keys = jnp.concatenate([block_of(k_ref, klist_ref[base + i]) for i in range(STEP)], axis=0)
         s = scores_of(keys, h)
         for i in range(STEP):
             part = s[:, i * BLOCK : (i + 1) * BLOCK]
-            bufs[h % 2][t * CHUNK + u + i] = part
+            bufs[h % 2][slot + i] = part
             top = jnp.maximum(top, part)
         return top
 
-    def value_part(h, t, u, m, total, acc):
-        base = (turn * heads + h) * list_len + t * CHUNK + u
+    def value_part(h, slot, m, total, acc):
+        base = (turn * heads + h) * list_len + slot
         values = jnp.concatenate([block_of(v_ref, klist_ref[base + i]) for i in range(STEP)], axis=0)
         parts = [jnp.exp2(bufs[h % 2][slist_ref[base + i]] - m) for i in range(STEP)]
         for p in parts:
@@ -84,36 +85,36 @@
 
     top_start = jnp.full((BLOCK, BLOCK), NEG_FILL, jnp.float32)
 
-    def first(t, top):
-        for u in range(0, CHUNK, STEP):
-            top = score_part(0, t, u, top)
-        return top
-
-    top = lax.fori_loop(0, chunks[0], first, top_start)
+    def walk(halves, visit, carry):
+        wide = CHUNK // HALF
+
+        def run(start, size, carry):
+            for u in range(0, size, STEP):
+                carry = visit(start + u, carry)
+            return carry
+
+        carry = lax.fori_loop(0, halves // wide, lambda t, c: run(t * CHUNK, CHUNK, c), carry)
+        return lax.fori_loop(halves // wide * wide, halves, lambda t, c: run(t * HALF, HALF, c), carry)
+
+    top = walk(chunks[0], lambda slot, top: score_part(0, slot, top), top_start)
     zeros = jnp.zeros((BLOCK, BLOCK), jnp.float32)
     for h in range(heads):
         top = jnp.maximum(jnp.where(counts[h] > 0, top, NEG_FILL), diag_sc[h])
         m = jnp.max(top, axis=1, keepdims=True)
         if h + 1 < heads:
 
-            def both(t, carry, h=h, m=m):
+            def both(slot, carry, h=h, m=m):
                 top, total, acc = carry
-                for u in range(0, CHUNK, STEP):
-                    top = score_part(h + 1, t, u, top)
-                    total, acc = value_part(h, t, u, m, total, acc)
-                return top, total, acc
-
-            top, total, acc = lax.fori_loop(
-                0, jnp.maximum(chunks[h], chunks[h + 1]), both, (top_start, zeros, zeros)
-            )
+                top = score_part(h + 1, slot, top)
+                return (top,) + value_part(h, slot, m, total, acc)
+
+            top, total, acc = walk(jnp.maximum(chunks[h], chunks[h + 1]), both, (top_start, zeros, zeros))
         else:
 
-            def last(t, carry, h=h, m=m):
-                for u in range(0, CHUNK, STEP):
-                    carry = value_part(h, t, u, m, *carry)
-                return carry
-
-            total, acc = lax.fori_loop(0, chunks[h], last, (zeros, zeros))
+            def last(slot, carry, h=h, m=m):
+                return value_part(h, slot, m, *carry)
+
+            total, acc = walk(chunks[h], last, (zeros, zeros))
         m_sc[h] = jnp.broadcast_to(m, (BLOCK, BLOCK))
         total_sc[h] = total
         acc_sc[h] = acc
@@ -290,19 +291,13 @@
         return lax.ppermute(x, "ctx", [(i, i ^ mask) for i in range(ctx_count)]) if mask else x
 
     q_own = jnp.concatenate(
-        [
-            swap(lax.dynamic_slice_in_dim(queries, (mine ^ m) * feats, feats, 1), m)
-            for m in range(plane)
-        ],
+        [swap(lax.dynamic_slice_in_dim(queries, (mine ^ m) * feats, feats, 1), m) for m in range(plane)],
         axis=0,
     )
 
     def by_head(cache):
         heads_first = lax.optimization_barrier(jnp.transpose(cache, (1, 0, 2)))
-        moved = [
-            swap(lax.dynamic_index_in_dim(heads_first, mine ^ m, 0, keepdims=False), m)
-            for m in range(plane)
-        ]
+        moved = [swap(lax.dynamic_index_in_dim(heads_first, mine ^ m, 0, keepdims=False), m) for m in range(plane)]
         return jnp.concatenate(moved, axis=0)
 
     q_parts = []
@@ -317,11 +312,7 @@
         lax.dynamic_slice_in_dim(slash_offsets, mine * heads, heads, 0),
         all_blocks - lines + turns,
         jnp.concatenate(
-            [
-                (place ^ m) * (local_len // BLOCK)
-                + jnp.arange(local_len // BLOCK, dtype=jnp.int32)
-                for m in range(plane)
-            ]
+            [(place ^ m) * (local_len // BLOCK) + jnp.arange(local_len // BLOCK, dtype=jnp.int32) for m in range(plane)]
         ),
     )
     source = (turns[:, None] * plane + jnp.arange(plane, dtype=jnp.int32)[None, :]) ^ place
@@ -331,7 +322,7 @@
     half = jnp.where(core + steps >= core_count, core + steps - core_count, core + steps)
     order = (half[:, None] * share + jnp.arange(share, dtype=jnp.int32)[None, :]).reshape(-1) ^ line
 
-    visits = ([2, 3, 1] + list(range(4, lines)) if lines >= 4 else list(range(1, lines))) + [0]
+    visits = ([2, 1, 3] + list(range(4, lines)) if lines >= 4 else list(range(1, lines))) + [0]
     keys, values, weight, table, order, meta, q_parts[visits[0]] = lax.optimization_barrier(
         (keys, values, out_weight, table, order, meta, q_parts[visits[0]])
     )

time: 170 us -> 160 us (0.941)
  waiting for transfers between devices: 80.3 us -> 68.9 us
  starting transfers between devices: 51.8 us -> 54.5 us
    ppermute x24, waiting for transfers between devices: 77.7 us -> 66.3 us  [swap(): lax.ppermute(x, 'ctx', [(i, i ^ mask) for i in range(ctx_count)])]
    ppermute x24, starting transfers between devices: 51.7 us -> 54.4 us  [swap(): lax.ppermute(x, 'ctx', [(i, i ^ mask) for i in range(ctx_count)])]
  transfers between devices with their start and end apart: 25 -> 25, of which waited for: 12 -> 14; matrix products, arithmetic and copies ran while one was open for 5% -> 6% of each run, Pallas kernels for 10% -> 10%
where the time goes in v2:
time: 160 us
  waiting for transfers between devices  68.9 us (43%)
  starting transfers between devices  54.5 us (34%)
  Pallas kernels  24 us (15%)
  other arithmetic  7.55 us (5%)
  local copies, waits for them, and re-layouts  4.85 us (3%)
    ppermute x24, waiting for transfers between devices, swap(): lax.ppermute(x, 'ctx', [(i, i ^ mask) for i in range(ctx_count)])  66.3 us
    ppermute x24, starting transfers between devices, swap(): lax.ppermute(x, 'ctx', [(i, i ^ mask) for i in range(ctx_count)])  54.4 us
    pallas_call x4, Pallas kernels, block_attention(): pl.pallas_call(partial(attention_kernel, scale2=float(width) ** (-0.5) *...  20.1 us
  transfers between devices with their start and end apart: 25, of which 14 were waited for; matrix products, arithmetic and copies ran while one was open for 6% of the time, Pallas kernels for 10%

profile of v2, /device:TPU:0, one launch (start us, length us, event | category | flops | bytes accessed | tf_op | source)
XLA Modules:
  0.0 160.1 jit_solution(12212513165462515890)
XLA Ops:
  1.6 3.0 %collective-permute-start.6 = (bf16[32,1024]{1,0:T(8,128)(2,1)}, bf16[32,1024]{1,0:T(8,128)(2,1)}, u32[]{:S(2)}, u32[]{:S(2)}) collective-permute-start(bf16[32,1024]{1,0:T(8,128)(2,1)} %get-tuple-element.59), channel_id=1, source_target_pairs={{0,2},{2,0},{4,6},{6,4},{8,10},{10,8},{12,14},{14,12},{16,18},{18,... | collective-permute-start | bytes 196616 | tf_op jit(solution)/shard_map/ppermute | solution.py:291
  17.0 2.9 %collective-permute-start.5 = (bf16[1024,128]{1,0:T(8,128)(2,1)S(1)}, bf16[1024,128]{1,0:T(8,128)(2,1)S(1)}, u32[]{:S(2)}, u32[]{:S(2)}) collective-permute-start(bf16[1024,128]{1,0:T(8,128)(2,1)S(1)} %get-tuple-element.51), channel_id=1, source_target_pairs={{0,6},{2,4},{4,2},{6,0},{8,14},{10,12},{12,10},{14,8},{16,22},{18,... | collective-permute-start | bytes 786440 | tf_op jit(solution)/shard_map/ppermute | solution.py:291
  19.9 8.9 %collective-permute-done.7 = bf16[32,1024]{1,0:T(8,128)(2,1)S(1)} collective-permute-done((bf16[32,1024]{1,0:T(8,128)(2,1)}, bf16[32,1024]{1,0:T(8,128)(2,1)S(1)}, u32[]{:S(2)}, u32[]{:S(2)}) %collective-permute-start.7) | collective-permute-done | bytes 65568 | tf_op jit(solution)/shard_map/ppermute | solution.py:291
  31.7 3.6 %collective-permute-start.11 = (bf16[128,1024]{1,0:T(8,128)(2,1)S(1)}, bf16[128,1024]{1,0:T(8,128)(2,1)S(1)}, u32[]{:S(2)}, u32[]{:S(2)}) collective-permute-start(bf16[128,1024]{1,0:T(8,128)(2,1)S(1)} %pad_maximum_fusion.2.refs_0_), channel_id=1, source_target_pairs={{0,24},{2,26},{4,28},{6,30},{8,16},{10,18},{12,20},{14,22},{16,8},... | collective-permute-start | bytes 786440 | tf_op jit(solution)/shard_map/ppermute | solution.py:291
  38.7 18.5 %collective-permute-done.9.refs_0_ = bf16[128,1024]{1,0:T(8,128)(2,1)S(1)} collective-permute-done((bf16[128,1024]{1,0:T(8,128)(2,1)S(1)}, bf16[128,1024]{1,0:T(8,128)(2,1)S(1)}, u32[]{:S(2)}, u32[]{:S(2)}) %collective-permute-start.9) | collective-permute-done | bytes 262176 | tf_op jit(solution)/shard_map/ppermute | solution.py:291
  57.2 5.0 %block_attention.4 = bf16[128,1152]{1,0:T(8,128)(2,1)S(1)} custom-call(s32[1]{0:T(128)} %constant.63.clone.1.turn_ref, s32[32]{0:T(128)S(1)} %reshape.120.count_ref, s32[4]{0:T(128)S(1)} %broadcast_select_fusion.diag_ref, s32[1024]{0:T(1024)S(1)} %reshape.121.klist_ref, s32[1024]{0:T(1024)S(1)} %compare_select_fusion.slist_ref, s32[16]{0:T(128)S(1)} %and.26.table_ref, ...), custom_call_target="tpu_custom_call" | custom-call | tf_op jit(solution)/shard_map/block_attention/pallas_call | solution.py:155
  62.3 5.0 %block_attention.5 = bf16[128,1152]{1,0:T(8,128)(2,1)S(1)} custom-call(s32[1]{0:T(128)} %constant.64.clone.1.turn_ref, s32[32]{0:T(128)S(1)} %reshape.120.count_ref, s32[4]{0:T(128)S(1)} %broadcast_select_fusion.diag_ref, s32[1024]{0:T(1024)S(1)} %reshape.121.klist_ref, s32[1024]{0:T(1024)S(1)} %compare_select_fusion.slist_ref, s32[16]{0:T(128)S(1)} %and.26.table_ref, ...), custom_call_target="tpu_custom_call" | custom-call | tf_op jit(solution)/shard_map/block_attention/pallas_call | solution.py:155
  67.3 5.0 %block_attention.6 = bf16[128,1152]{1,0:T(8,128)(2,1)S(1)} custom-call(s32[1]{0:T(128)} %constant.65.clone.1.turn_ref, s32[32]{0:T(128)S(1)} %reshape.120.count_ref, s32[4]{0:T(128)S(1)} %broadcast_select_fusion.diag_ref, s32[1024]{0:T(1024)S(1)} %reshape.121.klist_ref, s32[1024]{0:T(1024)S(1)} %compare_select_fusion.slist_ref, s32[16]{0:T(128)S(1)} %and.26.table_ref, ...), custom_call_target="tpu_custom_call" | custom-call | tf_op jit(solution)/shard_map/block_attention/pallas_call | solution.py:155
  72.3 11.3 %collective-permute-start.14 = (bf16[128,1152]{1,0:T(8,128)(2,1)S(1)}, bf16[128,1152]{1,0:T(8,128)(2,1)S(1)}, u32[]{:S(2)}, u32[]{:S(2)}) collective-permute-start(bf16[128,1152]{1,0:T(8,128)(2,1)S(1)} %block_attention.6), channel_id=1, source_target_pairs={{0,24},{2,26},{4,28},{6,30},{8,16},{10,18},{12,20},{14,22},{16,8},... | collective-permute-start | bytes 884744 | tf_op jit(solution)/shard_map/ppermute | solution.py:291
  83.9 3.7 %collective-permute-start.20 = (bf16[1024,512]{1,0:T(8,128)(2,1)S(1)}, bf16[1024,512]{1,0:T(8,128)(2,1)S(1)}, u32[]{:S(2)}, u32[]{:S(2)}) collective-permute-start(bf16[1024,512]{1,0:T(8,128)(2,1)S(1)} %get-tuple-element.43), channel_id=1, source_target_pairs={{0,6},{2,4},{4,2},{6,0},{8,14},{10,12},{12,10},{14,8},{16,22},{18,... | collective-permute-start | bytes 3145736 | tf_op jit(solution)/shard_map/ppermute | solution.py:291
  87.5 2.7 %collective-permute-start.19 = (bf16[1024,512]{1,0:T(8,128)(2,1)S(1)}, bf16[1024,512]{1,0:T(8,128)(2,1)S(1)}, u32[]{:S(2)}, u32[]{:S(2)}) collective-permute-start(bf16[1024,512]{1,0:T(8,128)(2,1)S(1)} %get-tuple-element.44), channel_id=1, source_target_pairs={{0,4},{2,6},{4,0},{6,2},{8,12},{10,14},{12,8},{14,10},{16,20},{18,... | collective-permute-start | bytes 3145736 | tf_op jit(solution)/shard_map/ppermute | solution.py:291
  91.5 5.1 %block_attention.7.refs_0_ = bf16[128,1152]{1,0:T(8,128)(2,1)S(1)} custom-call(s32[1]{0:T(128)} %constant.62.clone.1.turn_ref, s32[32]{0:T(128)S(1)} %reshape.120.count_ref, s32[4]{0:T(128)S(1)} %broadcast_select_fusion.diag_ref, s32[1024]{0:T(1024)S(1)} %reshape.121.klist_ref, s32[1024]{0:T(1024)S(1)} %compare_select_fusion.slist_ref, ...), custom_call_target="tpu_custom_call" | custom-call | tf_op jit(solution)/shard_map/block_attention/pallas_call | solution.py:155
  96.6 4.0 %collective-permute-done.12.refs_1_ = bf16[128,1152]{1,0:T(8,128)(2,1)S(1)} collective-permute-done((bf16[128,1152]{1,0:T(8,128)(2,1)S(1)}, bf16[128,1152]{1,0:T(8,128)(2,1)S(1)}, u32[]{:S(2)}, u32[]{:S(2)}) %collective-permute-start.12) | collective-permute-done | bytes 294944 | tf_op jit(solution)/shard_map/ppermute | solution.py:291
  100.6 6.4 %collective-permute-done.13.refs_2_ = bf16[128,1152]{1,0:T(8,128)(2,1)S(1)} collective-permute-done((bf16[128,1152]{1,0:T(8,128)(2,1)S(1)}, bf16[128,1152]{1,0:T(8,128)(2,1)S(1)}, u32[]{:S(2)}, u32[]{:S(2)}) %collective-permute-start.13) | collective-permute-done | bytes 294944 | tf_op jit(solution)/shard_map/ppermute | solution.py:291
  107.7 3.7 %collective-permute-start.17 = (bf16[128,1024]{1,0:T(8,128)(2,1)S(1)}, bf16[128,1024]{1,0:T(8,128)(2,1)S(1)}, u32[]{:S(2)}, u32[]{:S(2)}) collective-permute-start(bf16[128,1024]{1,0:T(8,128)(2,1)S(1)} %combine.1.refs_0_), channel_id=1, source_target_pairs={{0,24},{2,26},{4,28},{6,30},{8,16},{10,18},{12,20},{14,22},{16,8},... | collective-permute-start | bytes 786440 | tf_op jit(solution)/shard_map/ppermute | solution.py:291
  111.4 7.4 %collective-permute-done.17.refs_3_ = bf16[128,1024]{1,0:T(8,128)(2,1)S(1)} collective-permute-done((bf16[128,1024]{1,0:T(8,128)(2,1)S(1)}, bf16[128,1024]{1,0:T(8,128)(2,1)S(1)}, u32[]{:S(2)}, u32[]{:S(2)}) %collective-permute-start.17) | collective-permute-done | bytes 262176 | tf_op jit(solution)/shard_map/ppermute | solution.py:291
  118.8 9.3 %collective-permute-start.15 = (bf16[128,1024]{1,0:T(8,128)(2,1)S(1)}, bf16[128,1024]{1,0:T(8,128)(2,1)S(1)}, u32[]{:S(2)}, u32[]{:S(2)}) collective-permute-start(bf16[128,1024]{1,0:T(8,128)(2,1)S(1)} %combine.1.refs_0_), channel_id=1, source_target_pairs={{0,8},{2,10},{4,12},{6,14},{8,0},{10,2},{12,4},{14,6},{16,24},{18,... | collective-permute-start | bytes 786440 | tf_op jit(solution)/shard_map/ppermute | solution.py:291
  128.2 2.4 %collective-permute-done.16.refs_2_ = bf16[128,1024]{1,0:T(8,128)(2,1)S(1)} collective-permute-done((bf16[128,1024]{1,0:T(8,128)(2,1)S(1)}, bf16[128,1024]{1,0:T(8,128)(2,1)S(1)}, u32[]{:S(2)}, u32[]{:S(2)}) %collective-permute-start.16) | collective-permute-done | bytes 262176 | tf_op jit(solution)/shard_map/ppermute | solution.py:291
  130.6 2.7 %collective-permute-done.15.refs_1_ = bf16[128,1024]{1,0:T(8,128)(2,1)S(1)} collective-permute-done((bf16[128,1024]{1,0:T(8,128)(2,1)S(1)}, bf16[128,1024]{1,0:T(8,128)(2,1)S(1)}, u32[]{:S(2)}, u32[]{:S(2)}) %collective-permute-start.15) | collective-permute-done | bytes 262176 | tf_op jit(solution)/shard_map/ppermute | solution.py:291
  133.6 3.1 %project.1 = (bf16[4,1,256,512]{3,2,1,0:T(8,128)(2,1)S(1)}, f32[4,256,512]{2,1,0:T(8,128)S(1)}) custom-call(s32[4]{0:T(128)S(1)} %xor.66.order_ref, bf16[128,1024]{1,0:T(8,128)(2,1)S(1)} %combine.1.refs_0_, bf16[128,1024]{1,0:T(8,128)(2,1)S(1)} %collective-permute-done.15.refs_1_, bf16[128,1024]{1,0:T(8,128)(2,1)S(1)} %collective-permute-done.16.refs_2_, ...), custom_call_target="tpu_custom_call" | custom-call | tf_op jit(solution)/shard_map/project/pallas_call | solution.py:232
  136.8 2.6 %collective-permute-done.21 = bf16[4,256,512]{2,1,0:T(8,128)(2,1)S(1)} collective-permute-done((bf16[4,256,512]{2,1,0:T(8,128)(2,1)S(1)}, bf16[4,256,512]{2,1,0:T(8,128)(2,1)S(1)}, u32[]{:S(2)}, u32[]{:S(2)}) %collective-permute-start.21) | collective-permute-done | bytes 1048608 | tf_op jit(solution)/shard_map/ppermute | solution.py:345
  141.8 3.8 %collective-permute-start.24 = (bf16[256,512]{1,0:T(8,128)(2,1)S(1)}, bf16[256,512]{1,0:T(8,128)(2,1)S(1)}, u32[]{:S(2)}, u32[]{:S(2)}) collective-permute-start(bf16[256,512]{1,0:T(8,128)(2,1)S(1)} %get-tuple-element.48), channel_id=1, source_target_pairs={{0,6},{2,4},{4,2},{6,0},{8,14},{10,12},{12,10},{14,8},{16,22},{18,... | collective-permute-start | bytes 786440 | tf_op jit(solution)/shard_map/ppermute | solution.py:291
  146.1 2.8 %collective-permute-done.22 = bf16[256,512]{1,0:T(8,128)(2,1)S(1)} collective-permute-done((bf16[256,512]{1,0:T(8,128)(2,1)S(1)}, bf16[256,512]{1,0:T(8,128)(2,1)S(1)}, u32[]{:S(2)}, u32[]{:S(2)}) %collective-permute-start.22) | collective-permute-done | bytes 262176 | tf_op jit(solution)/shard_map/ppermute | solution.py:291
  148.9 9.0 %collective-permute-done.24 = bf16[256,512]{1,0:T(8,128)(2,1)S(1)} collective-permute-done((bf16[256,512]{1,0:T(8,128)(2,1)S(1)}, bf16[256,512]{1,0:T(8,128)(2,1)S(1)}, u32[]{:S(2)}, u32[]{:S(2)}) %collective-permute-start.24) | collective-permute-done | bytes 262176 | tf_op jit(solution)/shard_map/ppermute | solution.py:291
  (86 shorter events, 28.0 us)
Async XLA Ops:
  1.6 14.1 %collective-permute-start.6 = (bf16[32,1024]{1,0:T(8,128)(2,1)}, bf16[32,1024]{1,0:T(8,128)(2,1)}, u32[]{:S(2)}, u32[]{:S(2)}) collective-permute-start(bf16[32,1024]{1,0:T(8,128)(2,1)} %get-tuple-element.59), channel_id=1, source_target_pairs={{0,2},{2,0},{4,6},{6,4},{8,10},{10,8},{12,14},{14,12},{16,18},{18,... | collective-permute-start | bytes 196616 | tf_op jit(solution)/shard_map/ppermute | solution.py:291
  4.6 12.4 %collective-permute-start.8 = (bf16[32,1024]{1,0:T(8,128)(2,1)}, bf16[32,1024]{1,0:T(8,128)(2,1)}, u32[]{:S(2)}, u32[]{:S(2)}) collective-permute-start(bf16[32,1024]{1,0:T(8,128)(2,1)} %get-tuple-element.60), channel_id=1, source_target_pairs={{0,6},{2,4},{4,2},{6,0},{8,14},{10,12},{12,10},{14,8},{16,22},{18,... | collective-permute-start | bytes 196616 | tf_op jit(solution)/shard_map/ppermute | solution.py:291
  7.7 23.0 %collective-permute-start.2 = (bf16[1024,128]{1,0:T(8,128)(2,1)S(1)}, bf16[1024,128]{1,0:T(8,128)(2,1)S(1)}, u32[]{:S(2)}, u32[]{:S(2)}) collective-permute-start(bf16[1024,128]{1,0:T(8,128)(2,1)S(1)} %get-tuple-element.55), channel_id=1, source_target_pairs={{0,6},{2,4},{4,2},{6,0},{8,14},{10,12},{12,10},{14,8},{16,22},{18,... | collective-permute-start | bytes 786440 | tf_op jit(solution)/shard_map/ppermute | solution.py:291
  9.2 22.6 %collective-permute-start.1 = (bf16[1024,128]{1,0:T(8,128)(2,1)S(1)}, bf16[1024,128]{1,0:T(8,128)(2,1)}, u32[]{:S(2)}, u32[]{:S(2)}) collective-permute-start(bf16[1024,128]{1,0:T(8,128)(2,1)S(1)} %get-tuple-element.56), channel_id=1, source_target_pairs={{0,4},{2,6},{4,0},{6,2},{8,12},{10,14},{12,8},{14,10},{16,20},{18,... | collective-permute-start | bytes 786440 | tf_op jit(solution)/shard_map/ppermute | solution.py:291
  10.7 24.6 %collective-permute-start = (bf16[1024,128]{1,0:T(8,128)(2,1)S(1)}, bf16[1024,128]{1,0:T(8,128)(2,1)}, u32[]{:S(2)}, u32[]{:S(2)}) collective-permute-start(bf16[1024,128]{1,0:T(8,128)(2,1)S(1)} %get-tuple-element.57), channel_id=1, source_target_pairs={{0,2},{2,0},{4,6},{6,4},{8,10},{10,8},{12,14},{14,12},{16,18},{18,... | collective-permute-start | bytes 786440 | tf_op jit(solution)/shard_map/ppermute | solution.py:291
  15.7 13.0 %collective-permute-start.7 = (bf16[32,1024]{1,0:T(8,128)(2,1)}, bf16[32,1024]{1,0:T(8,128)(2,1)S(1)}, u32[]{:S(2)}, u32[]{:S(2)}) collective-permute-start(bf16[32,1024]{1,0:T(8,128)(2,1)} %get-tuple-element.61), channel_id=1, source_target_pairs={{0,4},{2,6},{4,0},{6,2},{8,12},{10,14},{12,8},{14,10},{16,20},{18,... | collective-permute-start | bytes 196616 | tf_op jit(solution)/shard_map/ppermute | solution.py:291
  17.0 19.4 %collective-permute-start.5 = (bf16[1024,128]{1,0:T(8,128)(2,1)S(1)}, bf16[1024,128]{1,0:T(8,128)(2,1)S(1)}, u32[]{:S(2)}, u32[]{:S(2)}) collective-permute-start(bf16[1024,128]{1,0:T(8,128)(2,1)S(1)} %get-tuple-element.51), channel_id=1, source_target_pairs={{0,6},{2,4},{4,2},{6,0},{8,14},{10,12},{12,10},{14,8},{16,22},{18,... | collective-permute-start | bytes 786440 | tf_op jit(solution)/shard_map/ppermute | solution.py:291
  28.7 8.5 %collective-permute-start.4 = (bf16[1024,128]{1,0:T(8,128)(2,1)S(1)}, bf16[1024,128]{1,0:T(8,128)(2,1)S(1)}, u32[]{:S(2)}, u32[]{:S(2)}) collective-permute-start(bf16[1024,128]{1,0:T(8,128)(2,1)S(1)} %get-tuple-element.52), channel_id=1, source_target_pairs={{0,4},{2,6},{4,0},{6,2},{8,12},{10,14},{12,8},{14,10},{16,20},{18,... | collective-permute-start | bytes 786440 | tf_op jit(solution)/shard_map/ppermute | solution.py:291
  30.7 8.0 %collective-permute-start.3 = (bf16[1024,128]{1,0:T(8,128)(2,1)S(1)}, bf16[1024,128]{1,0:T(8,128)(2,1)S(1)}, u32[]{:S(2)}, u32[]{:S(2)}) collective-permute-start(bf16[1024,128]{1,0:T(8,128)(2,1)S(1)} %get-tuple-element.53), channel_id=1, source_target_pairs={{0,2},{2,0},{4,6},{6,4},{8,10},{10,8},{12,14},{14,12},{16,18},{18,... | collective-permute-start | bytes 786440 | tf_op jit(solution)/shard_map/ppermute | solution.py:291
  31.7 35.6 %collective-permute-start.11 = (bf16[128,1024]{1,0:T(8,128)(2,1)S(1)}, bf16[128,1024]{1,0:T(8,128)(2,1)S(1)}, u32[]{:S(2)}, u32[]{:S(2)}) collective-permute-start(bf16[128,1024]{1,0:T(8,128)(2,1)S(1)} %pad_maximum_fusion.2.refs_0_), channel_id=1, source_target_pairs={{0,24},{2,26},{4,28},{6,30},{8,16},{10,18},{12,20},{14,22},{16,8},... | collective-permute-start | bytes 786440 | tf_op jit(solution)/shard_map/ppermute | solution.py:291
  35.3 27.0 %collective-permute-start.10 = (bf16[128,1024]{1,0:T(8,128)(2,1)S(1)}, bf16[128,1024]{1,0:T(8,128)(2,1)S(1)}, u32[]{:S(2)}, u32[]{:S(2)}) collective-permute-start(bf16[128,1024]{1,0:T(8,128)(2,1)S(1)} %pad_maximum_fusion.2.refs_0_), channel_id=1, source_target_pairs={{0,8},{2,10},{4,12},{6,14},{8,0},{10,2},{12,4},{14,6},{16,24},{18,... | collective-permute-start | bytes 786440 | tf_op jit(solution)/shard_map/ppermute | solution.py:291
  36.4 20.8 %collective-permute-start.9 = (bf16[128,1024]{1,0:T(8,128)(2,1)S(1)}, bf16[128,1024]{1,0:T(8,128)(2,1)S(1)}, u32[]{:S(2)}, u32[]{:S(2)}) collective-permute-start(bf16[128,1024]{1,0:T(8,128)(2,1)S(1)} %pad_maximum_fusion.2.refs_0_), channel_id=1, source_target_pairs={{0,16},{2,18},{4,20},{6,22},{8,24},{10,26},{12,28},{14,30},{16,0},... | collective-permute-start | bytes 786440 | tf_op jit(solution)/shard_map/ppermute | solution.py:291
  72.3 19.1 %collective-permute-start.14 = (bf16[128,1152]{1,0:T(8,128)(2,1)S(1)}, bf16[128,1152]{1,0:T(8,128)(2,1)S(1)}, u32[]{:S(2)}, u32[]{:S(2)}) collective-permute-start(bf16[128,1152]{1,0:T(8,128)(2,1)S(1)} %block_attention.6), channel_id=1, source_target_pairs={{0,24},{2,26},{4,28},{6,30},{8,16},{10,18},{12,20},{14,22},{16,8},... | collective-permute-start | bytes 884744 | tf_op jit(solution)/shard_map/ppermute | solution.py:291
  83.9 49.5 %collective-permute-start.20 = (bf16[1024,512]{1,0:T(8,128)(2,1)S(1)}, bf16[1024,512]{1,0:T(8,128)(2,1)S(1)}, u32[]{:S(2)}, u32[]{:S(2)}) collective-permute-start(bf16[1024,512]{1,0:T(8,128)(2,1)S(1)} %get-tuple-element.43), channel_id=1, source_target_pairs={{0,6},{2,4},{4,2},{6,0},{8,14},{10,12},{12,10},{14,8},{16,22},{18,... | collective-permute-start | bytes 3145736 | tf_op jit(solution)/shard_map/ppermute | solution.py:291
  87.5 46.0 %collective-permute-start.19 = (bf16[1024,512]{1,0:T(8,128)(2,1)S(1)}, bf16[1024,512]{1,0:T(8,128)(2,1)S(1)}, u32[]{:S(2)}, u32[]{:S(2)}) collective-permute-start(bf16[1024,512]{1,0:T(8,128)(2,1)S(1)} %get-tuple-element.44), channel_id=1, source_target_pairs={{0,4},{2,6},{4,0},{6,2},{8,12},{10,14},{12,8},{14,10},{16,20},{18,... | collective-permute-start | bytes 3145736 | tf_op jit(solution)/shard_map/ppermute | solution.py:291
  90.3 43.3 %collective-permute-start.18 = (bf16[1024,512]{1,0:T(8,128)(2,1)S(1)}, bf16[1024,512]{1,0:T(8,128)(2,1)S(1)}, u32[]{:S(2)}, u32[]{:S(2)}) collective-permute-start(bf16[1024,512]{1,0:T(8,128)(2,1)S(1)} %get-tuple-element.45), channel_id=1, source_target_pairs={{0,2},{2,0},{4,6},{6,4},{8,10},{10,8},{12,14},{14,12},{16,18},{18,... | collective-permute-start | bytes 3145736 | tf_op jit(solution)/shard_map/ppermute | solution.py:291
  90.3 10.3 %collective-permute-start.12 = (bf16[128,1152]{1,0:T(8,128)(2,1)S(1)}, bf16[128,1152]{1,0:T(8,128)(2,1)S(1)}, u32[]{:S(2)}, u32[]{:S(2)}) collective-permute-start(bf16[128,1152]{1,0:T(8,128)(2,1)S(1)} %block_attention.5), channel_id=1, source_target_pairs={{0,8},{2,10},{4,12},{6,14},{8,0},{10,2},{12,4},{14,6},{16,24},{18,... | collective-permute-start | bytes 884744 | tf_op jit(solution)/shard_map/ppermute | solution.py:291
  91.5 15.5 %collective-permute-start.13 = (bf16[128,1152]{1,0:T(8,128)(2,1)S(1)}, bf16[128,1152]{1,0:T(8,128)(2,1)S(1)}, u32[]{:S(2)}, u32[]{:S(2)}) collective-permute-start(bf16[128,1152]{1,0:T(8,128)(2,1)S(1)} %block_attention.4), channel_id=1, source_target_pairs={{0,16},{2,18},{4,20},{6,22},{8,24},{10,26},{12,28},{14,30},{16,0},... | collective-permute-start | bytes 884744 | tf_op jit(solution)/shard_map/ppermute | solution.py:291
  107.7 11.1 %collective-permute-start.17 = (bf16[128,1024]{1,0:T(8,128)(2,1)S(1)}, bf16[128,1024]{1,0:T(8,128)(2,1)S(1)}, u32[]{:S(2)}, u32[]{:S(2)}) collective-permute-start(bf16[128,1024]{1,0:T(8,128)(2,1)S(1)} %combine.1.refs_0_), channel_id=1, source_target_pairs={{0,24},{2,26},{4,28},{6,30},{8,16},{10,18},{12,20},{14,22},{16,8},... | collective-permute-start | bytes 786440 | tf_op jit(solution)/shard_map/ppermute | solution.py:291
  111.4 19.2 %collective-permute-start.16 = (bf16[128,1024]{1,0:T(8,128)(2,1)S(1)}, bf16[128,1024]{1,0:T(8,128)(2,1)S(1)}, u32[]{:S(2)}, u32[]{:S(2)}) collective-permute-start(bf16[128,1024]{1,0:T(8,128)(2,1)S(1)} %combine.1.refs_0_), channel_id=1, source_target_pairs={{0,16},{2,18},{4,20},{6,22},{8,24},{10,26},{12,28},{14,30},{16,0},... | collective-permute-start | bytes 786440 | tf_op jit(solution)/shard_map/ppermute | solution.py:291
  118.8 14.5 %collective-permute-start.15 = (bf16[128,1024]{1,0:T(8,128)(2,1)S(1)}, bf16[128,1024]{1,0:T(8,128)(2,1)S(1)}, u32[]{:S(2)}, u32[]{:S(2)}) collective-permute-start(bf16[128,1024]{1,0:T(8,128)(2,1)S(1)} %combine.1.refs_0_), channel_id=1, source_target_pairs={{0,8},{2,10},{4,12},{6,14},{8,0},{10,2},{12,4},{14,6},{16,24},{18,... | collective-permute-start | bytes 786440 | tf_op jit(solution)/shard_map/ppermute | solution.py:291
  140.0 8.9 %collective-permute-start.22 = (bf16[256,512]{1,0:T(8,128)(2,1)S(1)}, bf16[256,512]{1,0:T(8,128)(2,1)S(1)}, u32[]{:S(2)}, u32[]{:S(2)}) collective-permute-start(bf16[256,512]{1,0:T(8,128)(2,1)S(1)} %get-tuple-element.47), channel_id=1, source_target_pairs={{0,2},{2,0},{4,6},{6,4},{8,10},{10,8},{12,14},{14,12},{16,18},{18,... | collective-permute-start | bytes 786440 | tf_op jit(solution)/shard_map/ppermute | solution.py:291
  141.8 16.0 %collective-permute-start.24 = (bf16[256,512]{1,0:T(8,128)(2,1)S(1)}, bf16[256,512]{1,0:T(8,128)(2,1)S(1)}, u32[]{:S(2)}, u32[]{:S(2)}) collective-permute-start(bf16[256,512]{1,0:T(8,128)(2,1)S(1)} %get-tuple-element.48), channel_id=1, source_target_pairs={{0,6},{2,4},{4,2},{6,0},{8,14},{10,12},{12,10},{14,8},{16,22},{18,... | collective-permute-start | bytes 786440 | tf_op jit(solution)/shard_map/ppermute | solution.py:291
  145.6 13.7 %collective-permute-start.23 = (bf16[256,512]{1,0:T(8,128)(2,1)S(1)}, bf16[256,512]{1,0:T(8,128)(2,1)S(1)}, u32[]{:S(2)}, u32[]{:S(2)}) collective-permute-start(bf16[256,512]{1,0:T(8,128)(2,1)S(1)} %get-tuple-element.49), channel_id=1, source_target_pairs={{0,4},{2,6},{4,0},{6,2},{8,12},{10,14},{12,8},{14,10},{16,20},{18,... | collective-permute-start | bytes 786440 | tf_op jit(solution)/shard_map/ppermute | solution.py:291
  (7 other events, 53.4 us)
